TPU v7x, 32 devices: a whole 2x2x4 slice. The times are simulated.
32 devices in a mesh: expert: 8 (over y, x, core), dp: 4 (over z).
Axes of the slice: x: 2, y: 2, z: 4, core: 2. Of those that a mesh axis runs over, the one named last changes fastest.
Arguments:
- tokens: bfloat16 [4096, 2048], P(('expert', 'dp')), may hold values from -6 to 6
- expert_ids: int32 [4096, 4], P(('expert', 'dp')), may hold values from 0 to 15, all different within a row; in each aligned block of 128 rows (0 to 127, 128 to 255, ...) at most 96 rows name the same one
- gate_probs: float32 [4096, 4], P(('expert', 'dp')), may hold values from 0.05 to 0.5
- expert_weights: bfloat16 [2048, 3, 16, 384], P(None, None, 'expert'), may hold values from -0.125 to 0.125
- out_grad: bfloat16 [4096, 2048], P(('expert', 'dp')), may hold values from -1.5 to 1.5
Outputs:
- layer_out: bfloat16 [4096, 2048], P(('expert', 'dp'))
- token_grad: bfloat16 [4096, 2048], P(('expert', 'dp'))
- gate_grad: float32 [4096, 4], P(('expert', 'dp'))
- weight_grad: float32 [2048, 3, 16, 384], P('dp', None, 'expert')
Inputs may be any that keep to these rules, and one draw needn't show every extreme that they name: `expert_ids`: each row names 4 different experts. Among the 128 rows of one device (aligned blocks of rows), no expert is named by more than 96 rows, and in some block some expert is named by exactly 96 rows.
All inputs are finite; a program needn't handle non-finite values.
Results may differ from a plain program's by a relative error of at most 0.0085.
Values may be sent and summed in bfloat16 or wider, within the bound.
A program may use at most 128 MiB of HBM per device.

v0:
```python
import jax
import jax.numpy as jnp
from jax import lax
from jax.sharding import PartitionSpec as P


def slot_tables(expert_ids, capacity, expert_count):
    tok_count, top_count = expert_ids.shape
    pair_count = tok_count * top_count
    flat_ids = expert_ids.reshape(pair_count)
    one_hot = (flat_ids[:, None] == jnp.arange(expert_count, dtype=jnp.int32)[None, :]).astype(
        jnp.int32
    )
    earlier = jnp.cumsum(one_hot, axis=0) - one_hot
    slot_rank = jnp.sum(earlier * one_hot, axis=1)
    slot_key = flat_ids * capacity + slot_rank
    matches = slot_key[None, :] == jnp.arange(expert_count * capacity, dtype=jnp.int32)[:, None]
    source_pair = (
        jnp.sum(jnp.where(matches, jnp.arange(pair_count, dtype=jnp.int32)[None, :] + 1, 0), axis=1)
        - 1
    )
    return (slot_key, source_pair)


def expert_hidden(row_block, expert_weights):
    gate_pre = jnp.einsum(
        "sicd,dih->sich", row_block, expert_weights[:, 0], preferred_element_type=jnp.float32
    )
    up_pre = jnp.einsum(
        "sicd,dih->sich", row_block, expert_weights[:, 1], preferred_element_type=jnp.float32
    )
    hidden = (gate_pre * jax.nn.sigmoid(gate_pre) * up_pre).astype(jnp.bfloat16)
    return (gate_pre, up_pre, hidden)


def expert_output(hidden, expert_weights):
    output = jnp.einsum(
        "sich,dih->sicd", hidden, expert_weights[:, 2], preferred_element_type=jnp.float32
    )
    return output.astype(jnp.bfloat16)


def expert_backward(cot_block, gate_pre, up_pre, expert_weights):
    sigmoid_gate = jax.nn.sigmoid(gate_pre)
    silu_gate = gate_pre * sigmoid_gate
    hidden_cot = jnp.einsum(
        "sicd,dih->sich", cot_block, expert_weights[:, 2], preferred_element_type=jnp.float32
    )
    gate_cot = (
        hidden_cot * up_pre * sigmoid_gate * (1.0 + gate_pre * (1.0 - sigmoid_gate))
    ).astype(jnp.bfloat16)
    up_cot = (hidden_cot * silu_gate).astype(jnp.bfloat16)
    token_cot = jnp.einsum(
        "sich,dih->sicd", gate_cot, expert_weights[:, 0], preferred_element_type=jnp.float32
    ) + jnp.einsum(
        "sich,dih->sicd", up_cot, expert_weights[:, 1], preferred_element_type=jnp.float32
    )
    return (gate_cot, up_cot, token_cot.astype(jnp.bfloat16))


def weight_term(row_block, cot_block, hidden, gate_cot, up_cot):
    gate_term = jnp.einsum(
        "sicd,sich->dih", row_block, gate_cot, preferred_element_type=jnp.float32
    )
    up_term = jnp.einsum("sicd,sich->dih", row_block, up_cot, preferred_element_type=jnp.float32)
    down_term = jnp.einsum("sicd,sich->dih", cot_block, hidden, preferred_element_type=jnp.float32)
    return jnp.stack([gate_term, up_term, down_term], axis=1)


def forward_pass(send_rows, expert_weights):
    row_block = lax.all_to_all(send_rows, "expert", split_axis=0, concat_axis=0, tiled=True)
    gate_pre, up_pre, hidden = expert_hidden(row_block, expert_weights)
    sent_back = lax.all_to_all(
        expert_output(hidden, expert_weights), "expert", split_axis=0, concat_axis=0, tiled=True
    )
    return (sent_back, row_block, gate_pre, up_pre, hidden)


def local(tokens, expert_ids, gate_probs, expert_weights, out_grad):
    tok_count, top_count = expert_ids.shape
    pair_count = tok_count * top_count
    model_width = tokens.shape[1]
    expert_ranks = lax.axis_size("expert")
    local_experts = expert_weights.shape[2]
    expert_count = local_experts * expert_ranks
    capacity = 3 * pair_count // expert_count
    slot_key, source_pair = slot_tables(expert_ids, capacity, expert_count)
    filled = source_pair >= 0
    safe_pair = jnp.maximum(source_pair, 0)
    block_shape = (expert_ranks, local_experts, capacity, model_width)
    send_rows = jnp.where(
        filled[:, None], tokens[safe_pair // top_count], jnp.zeros((), jnp.bfloat16)
    ).reshape(block_shape)
    out_cot = (gate_probs[:, :, None] * out_grad[:, None, :].astype(jnp.float32)).astype(
        jnp.bfloat16
    )
    out_cot = out_cot.reshape(pair_count, model_width)
    cot_rows = jnp.where(filled[:, None], out_cot[safe_pair], jnp.zeros((), jnp.bfloat16)).reshape(
        block_shape
    )
    returned, kept_rows, kept_gate, kept_up, kept_hidden = forward_pass(send_rows, expert_weights)
    arrived = lax.all_to_all(cot_rows, "expert", split_axis=0, concat_axis=0, tiled=True)
    gate_cot, up_cot, token_cot = expert_backward(arrived, kept_gate, kept_up, expert_weights)
    cot_back = lax.all_to_all(token_cot, "expert", split_axis=0, concat_axis=0, tiled=True)
    rows_used, cot_used, hidden_used = (kept_rows, arrived, kept_hidden)
    out_pairs = returned.reshape(-1, model_width)[slot_key].reshape(
        tok_count, top_count, model_width
    )
    layer_out = jnp.sum(gate_probs[:, :, None] * out_pairs.astype(jnp.float32), axis=1).astype(
        jnp.bfloat16
    )
    gate_grad = jnp.einsum("tkd,td->tk", out_pairs, out_grad, preferred_element_type=jnp.float32)
    grad_term = weight_term(rows_used, cot_used, hidden_used, gate_cot, up_cot)
    weight_grad = lax.psum_scatter(
        grad_term.astype(jnp.bfloat16), "dp", scatter_dimension=0, tiled=True
    ).astype(jnp.float32)
    pair_grads = cot_back.reshape(-1, model_width)[slot_key].reshape(
        tok_count, top_count, model_width
    )
    token_grad = jnp.sum(pair_grads.astype(jnp.float32), axis=1).astype(jnp.bfloat16)
    return (layer_out, token_grad, gate_grad, weight_grad)


def solution(mesh):
    in_specs = (
        P(("expert", "dp"), None),
        P(("expert", "dp"), None),
        P(("expert", "dp"), None),
        P(None, None, "expert", None),
        P(("expert", "dp"), None),
    )
    out_specs = (
        P(("expert", "dp"), None),
        P(("expert", "dp"), None),
        P(("expert", "dp"), None),
        P("dp", None, "expert", None),
    )
    return jax.shard_map(local, mesh=mesh, in_specs=in_specs, out_specs=out_specs, check_vma=False)
```

profile of v0, /device:TPU:8, one launch (start us, length us, event | category | flops | bytes accessed | tf_op | source)
XLA Modules:
  0.0 420.8 jit_solution(6515216334452598551)
XLA Ops:
  11.3 4.2 %mul.87 = f32[128,4,2048]{2,1,0:T(4,128)} broadcast(bf16[128,2048]{1,0:T(8,128)(2,1)} %param.9), dimensions={0,2} | broadcast | bytes 4718592 | tf_op jit(solution)/shard_map/mul | solution.py:94
  15.5 5.3 %mul.88 = f32[512,2048]{1,0:T(8,128)} reshape(f32[128,4,2048]{2,1,0:T(4,128)} %mul.87) | data formatting | bytes 8388608 | tf_op jit(solution)/shard_map/mul | solution.py:94
  20.8 2.5 multiply_convert_fusion
  23.2 7.1 %gather_fusion.2 = bf16[1536,2048]{1,0:T(8,128)(2,1)} fusion(bf16[512,2048]{1,0:T(8,128)(2,1)S(1)} %multiply_convert_fusion, s32[2048]{0:T(1024)S(1)} %pad_clamp_fusion), kind=kCustom, calls=%fused_computation.2 | custom fusion | bytes 12589056 | tf_op jit(solution)/shard_map/gather | solution.py:98
  30.3 7.1 %gather_fusion = bf16[1536,2048]{1,0:T(8,128)(2,1)} fusion(bf16[128,2048]{1,0:T(8,128)(2,1)S(1)} %copy-done, s32[2048]{0:T(1024)S(1)} %pad_clamp_fusion.1), kind=kCustom, calls=%fused_computation | custom fusion | bytes 12589056 | tf_op jit(solution)/shard_map/gather | solution.py:92
  37.4 8.2 %broadcast_select_fusion = (bf16[8,2,96,2048]{3,2,1,0:T(8,128)(2,1)}, bf16[8,2,96,2048]{3,2,1,0:T(8,128)(2,1)S(1)}) fusion(bf16[8,2,96,2048]{3,2,1,0:T(8,128)(2,1)} %bitcast.126, pred[8,2,96]{2,1,0:T(4,128)(4,1)S(1)} %ge.11, bf16[8,2,96,2048]{3,2,1,0:T(8,128)(2,1)} %bitcast.127), kind=kLoop, calls=%fused_computation.11 | loop fusion | flops 6291456 | bytes 25167360 | tf_op jit(solution)/shard_map/jit(_where)/select_n | solution.py:98
  45.6 75.2 %all_to_all.20 = bf16[8,2,96,2048]{3,2,1,0:T(8,128)(2,1)} all-to-all(bf16[8,2,96,2048]{3,2,1,0:T(8,128)(2,1)S(1)} %get-tuple-element.31), channel_id=1, replica_groups=mesh['expert'=8,'dp'=4] {'expert'}, dimensions={0} | all-to-all | bytes 12582912 | tf_op jit(solution)/shard_map/all_to_all | solution.py:71
  120.8 4.7 %all-to-all-start.2 = ((bf16[8,2,96,2048]{3,2,1,0:T(8,128)(2,1)}), bf16[8,2,96,2048]{3,2,1,0:T(8,128)(2,1)}, u32[]{:S(2)}, u32[]{:S(2)}) async-start(bf16[8,2,96,2048]{3,2,1,0:T(8,128)(2,1)} %get-tuple-element.30), calls=%async_computation.2 | async-start | bytes 12582912 | tf_op jit(solution)/shard_map/all_to_all | solution.py:102
  125.7 10.0 %fusion.46 = (bf16[2048,1,2,384]{3,2,1,0:T(2,128)(2,1)}, bf16[2048,1,2,384]{3,2,1,0:T(2,128)(2,1)S(1)}, bf16[2048,1,2,384]{3,2,1,0:T(2,128)(2,1)S(1)}) fusion(bf16[2048,3,2,384]{3,2,1,0:T(2,128)(2,1)} %param.8), kind=kLoop, calls=%fused_computation.78 | loop fusion | bytes 18874368 | tf_op jit(solution)/shard_map/slice | solution.py:38
  135.8 4.9 %fusion.9 = f32[2,8,96,384]{3,2,1,0:T(8,128)} fusion(bf16[8,2,96,2048]{3,2,1,0:T(8,128)(2,1)S(1)} %copy-done.5, bf16[2048,1,2,384]{3,2,1,0:T(2,128)(2,1)S(1)} %get-tuple-element.21), kind=kOutput, calls=%fused_computation.23 | convolution fusion | flops 2415919104 | bytes 11796480 | tf_op jit(solution)/shard_map/sicd,dih->sich/dot_general | solution.py:29
  140.7 4.8 %fusion.11 = f32[2,8,96,384]{3,2,1,0:T(8,128)} fusion(bf16[8,2,96,2048]{3,2,1,0:T(8,128)(2,1)S(1)} %copy-done.5, bf16[2048,1,2,384]{3,2,1,0:T(2,128)(2,1)S(1)} %get-tuple-element.22), kind=kOutput, calls=%fused_computation.25 | convolution fusion | flops 2415919104 | bytes 11796480 | tf_op jit(solution)/shard_map/sicd,dih->sich/dot_general | solution.py:26
  145.5 51.6 %all-to-all-done.2 = bf16[8,2,96,2048]{3,2,1,0:T(8,128)(2,1)} async-done(((bf16[8,2,96,2048]{3,2,1,0:T(8,128)(2,1)}), bf16[8,2,96,2048]{3,2,1,0:T(8,128)(2,1)}, u32[]{:S(2)}, u32[]{:S(2)}) %all-to-all-start.2) | async-done | bytes 6291488 | tf_op jit(solution)/shard_map/all_to_all | solution.py:102
  197.1 9.4 %fusion.32 = (bf16[8,2,96,384]{3,2,0,1:T(8,128)(2,1)S(1)}, bf16[8,2,96,384]{3,2,0,1:T(8,128)(2,1)S(1)}, bf16[8,2,96,384]{3,2,0,1:T(8,128)(2,1)S(1)}) fusion(f32[2,8,96,384]{3,2,1,0:T(8,128)} %fusion.11, f32[2,8,96,384]{3,2,1,0:T(8,128)} %fusion.9, bf16[2048,1,2,384]{3,2,1,0:T(2,128)(2,1)} %get-tuple-element.20, bf16[8,2,96,2048]{3,2,1,0:T(8,128)(2,1)} %all-to-all-done.2), kind=kOutput, calls=%fused_computation.41 | convolution fusion | flops 2424766464 | bytes 17694720 | tf_op jit(solution)/shard_map/sicd,dih->sich/dot_general | solution.py:46
  206.6 6.7 %fusion.25 = bf16[2048,1,2,384]{0,3,2,1:T(8,128)(2,1)S(1)} fusion(bf16[8,2,96,384]{3,2,0,1:T(8,128)(2,1)S(1)} %get-tuple-element.25, bf16[8,2,96,2048]{3,2,1,0:T(8,128)(2,1)} %all-to-all-done.2), kind=kOutput, calls=%fused_computation.34 | convolution fusion | flops 2417491968 | bytes 10616832 | tf_op jit(solution)/shard_map/sicd,sich->dih/dot_general | solution.py:66
  213.4 3.2 fusion.22
  216.5 2.9 fusion.19
  219.5 4.2 %pad_maximum_fusion = bf16[2048,3,2,384]{0,3,2,1:T(8,128)(2,1)} fusion(bf16[2048,1,2,384]{0,3,2,1:T(8,128)(2,1)S(1)} %fusion.25, bf16[2048,1,2,384]{0,3,2,1:T(8,128)(2,1)S(1)} %fusion.22, bf16[2048,1,2,384]{0,3,2,1:T(8,128)(2,1)S(1)} %fusion.19), kind=kLoop, calls=%fused_computation.5 | loop fusion | flops 9437184 | bytes 18874368 | tf_op jit(solution)/shard_map/stack | solution.py:67
  225.6 5.1 %convert_bitcast_fusion = bf16[8,2,96,2048]{3,2,0,1:T(8,128)(2,1)S(1)} fusion(bf16[8,2,96,384]{3,2,0,1:T(8,128)(2,1)} %copy-done.11, bf16[2048,1,2,384]{3,2,1,0:T(2,128)(2,1)S(1)} %copy-done.6), kind=kOutput, calls=%fused_computation.10 | convolution fusion | flops 2419064832 | bytes 10616832 | tf_op jit(solution)/shard_map/sich,dih->sicd/dot_general | solution.py:37
  230.8 3.2 copy.56
  233.9 4.7 %all-to-all-start.1 = ((bf16[8,2,96,2048]{3,2,1,0:T(8,128)(2,1)}), bf16[8,2,96,2048]{3,2,1,0:T(8,128)(2,1)}, u32[]{:S(2)}, u32[]{:S(2)}) async-start(bf16[8,2,96,2048]{3,2,1,0:T(8,128)(2,1)} %copy.56), calls=%async_computation.1 | async-start | bytes 12582912 | tf_op jit(solution)/shard_map/all_to_all | solution.py:73
  238.7 5.8 %fusion.28 = f32[2,8,96,2048]{3,2,1,0:T(8,128)S(1)} fusion(bf16[8,2,96,384]{3,2,0,1:T(8,128)(2,1)} %copy-done.8, bf16[2048,1,2,384]{3,2,1,0:T(2,128)(2,1)} %copy-done.2), kind=kOutput, calls=%fused_computation.35 | convolution fusion | flops 2415919104 | bytes 16908288 | tf_op jit(solution)/shard_map/sich,dih->sicd/dot_general | solution.py:53
  244.5 8.4 %fusion = bf16[8,2,96,2048]{3,2,0,1:T(8,128)(2,1)} fusion(f32[2,8,96,2048]{3,2,1,0:T(8,128)S(1)} %fusion.28, bf16[8,2,96,384]{3,2,0,1:T(8,128)(2,1)} %copy-done.7, bf16[2048,1,2,384]{3,2,1,0:T(2,128)(2,1)} %copy-done.3), kind=kOutput, calls=%fused_computation.6 | convolution fusion | flops 2422210560 | bytes 23199744 | tf_op jit(solution)/shard_map/sich,dih->sicd/dot_general | solution.py:55
  252.9 6.6 %copy.60 = bf16[8,2,96,2048]{3,2,1,0:T(8,128)(2,1)} copy(bf16[8,2,96,2048]{3,2,0,1:T(8,128)(2,1)} %fusion) | data formatting | bytes 12582912 | tf_op jit(solution)/shard_map/convert_element_type | solution.py:58
  259.5 50.8 %all-to-all-done.1 = bf16[8,2,96,2048]{3,2,1,0:T(8,128)(2,1)} async-done(((bf16[8,2,96,2048]{3,2,1,0:T(8,128)(2,1)}), bf16[8,2,96,2048]{3,2,1,0:T(8,128)(2,1)}, u32[]{:S(2)}, u32[]{:S(2)}) %all-to-all-start.1) | async-done | bytes 6291488 | tf_op jit(solution)/shard_map/all_to_all | solution.py:73
  310.3 5.2 %all-to-all-start.3 = ((bf16[8,2,96,2048]{3,2,1,0:T(8,128)(2,1)}), bf16[8,2,96,2048]{3,2,1,0:T(8,128)(2,1)}, u32[]{:S(2)}, u32[]{:S(2)}) async-start(bf16[8,2,96,2048]{3,2,1,0:T(8,128)(2,1)} %copy.60), calls=%async_computation.3 | async-start | bytes 12582912 | tf_op jit(solution)/shard_map/all_to_all | solution.py:104
  315.7 8.0 %gather_fusion.1 = bf16[512,2048]{1,0:T(8,128)(2,1)S(1)} fusion(bf16[1536,2048]{1,0:T(8,128)(2,1)} %bitcast.14, s32[1024]{0:T(1024)S(1)} %pad_clamp_fusion.2), kind=kCustom, calls=%fused_computation.1 | custom fusion | bytes 4196352 | tf_op jit(solution)/shard_map/gather | solution.py:106
  326.0 4.4 %fusion.38 = f32[128,1,4]{2,1,0:T(1,128)S(1)} fusion(bf16[128,4,2048]{2,1,0:T(4,128)(2,1)} %reshape.163, bf16[128,2048,1]{1,0,2:T(8,128)(2,1)S(1)} %bitcast.130), kind=kOutput, calls=%fused_computation.51 | convolution fusion | flops 2097152 | bytes 2623488 | tf_op jit(solution)/shard_map/tkd,td->tk/dot_general | solution.py:112
  331.0 56.0 %all-to-all-done.3 = bf16[8,2,96,2048]{3,2,1,0:T(8,128)(2,1)} async-done(((bf16[8,2,96,2048]{3,2,1,0:T(8,128)(2,1)}), bf16[8,2,96,2048]{3,2,1,0:T(8,128)(2,1)}, u32[]{:S(2)}, u32[]{:S(2)}) %all-to-all-start.3) | async-done | bytes 6291488 | tf_op jit(solution)/shard_map/all_to_all | solution.py:104
  387.1 8.0 %gather_fusion.3 = bf16[512,2048]{1,0:T(8,128)(2,1)S(1)} fusion(bf16[1536,2048]{1,0:T(8,128)(2,1)} %bitcast.23, s32[1024]{0:T(1024)S(1)} %pad_clamp_fusion.2), kind=kCustom, calls=%fused_computation.3 | custom fusion | bytes 4196352 | tf_op jit(solution)/shard_map/gather | solution.py:117
  397.4 5.1 %reduce_sum.45 = bf16[128,2048]{1,0:T(8,128)(2,1)} reduce(bf16[128,4,2048]{2,1,0:T(4,128)(2,1)} %reshape.165, bf16[]{:T(256)} %constant.39.clone.1), dimensions={1}, to_apply=%region_5.6 | reduce | flops 786432 | bytes 2621442 | tf_op jit(solution)/shard_map/reduce_sum | solution.py:120
  402.6 4.1 multiply_reduce_fusion
  406.7 7.1 %copy.64 = f32[512,3,2,384]{3,2,1,0:T(2,128)} copy(bf16[512,3,2,384]{0,3,2,1:T(8,128)(2,1)} %reduce-scatter.2.cloned.1.call-done) | data formatting | bytes 7077888
  (59 shorter events, 11.6 us)
Async XLA Ops:
  7.2 23.1 %copy-start = (bf16[128,2048]{1,0:T(8,128)(2,1)S(1)}, bf16[128,2048]{1,0:T(8,128)(2,1)}, u32[]{:S(2)}) copy-start(bf16[128,2048]{1,0:T(8,128)(2,1)} %param.5) | copy-start | bytes 1572868
  120.8 76.3 %all-to-all-start.2 = ((bf16[8,2,96,2048]{3,2,1,0:T(8,128)(2,1)}), bf16[8,2,96,2048]{3,2,1,0:T(8,128)(2,1)}, u32[]{:S(2)}, u32[]{:S(2)}) async-start(bf16[8,2,96,2048]{3,2,1,0:T(8,128)(2,1)} %get-tuple-element.30), calls=%async_computation.2 | async-start | bytes 12582912 | tf_op jit(solution)/shard_map/all_to_all | solution.py:102
  125.5 281.1 %reduce-scatter.2.cloned.1.call-start = ((), (), s32[]{:S(2)}) async-start(), calls=%async_computation.5 | async-start | bytes 11796480 | tf_op jit(solution)/shard_map/reduce_scatter | solution.py:114
  125.7 10.0 %copy-start.5 = (bf16[8,2,96,2048]{3,2,1,0:T(8,128)(2,1)S(1)}, bf16[8,2,96,2048]{3,2,1,0:T(8,128)(2,1)}, u32[]{:S(2)}) copy-start(bf16[8,2,96,2048]{3,2,1,0:T(8,128)(2,1)} %all_to_all.20) | copy-start | bytes 18874372
  135.8 5.0 %copy-start.3 = (bf16[2048,1,2,384]{3,2,1,0:T(2,128)(2,1)}, bf16[2048,1,2,384]{3,2,1,0:T(2,128)(2,1)S(1)}, u32[]{:S(2)}) copy-start(bf16[2048,1,2,384]{3,2,1,0:T(2,128)(2,1)S(1)} %get-tuple-element.21) | copy-start | bytes 9437188
  135.8 5.0 %copy-start.2 = (bf16[2048,1,2,384]{3,2,1,0:T(2,128)(2,1)}, bf16[2048,1,2,384]{3,2,1,0:T(2,128)(2,1)S(1)}, u32[]{:S(2)}) copy-start(bf16[2048,1,2,384]{3,2,1,0:T(2,128)(2,1)S(1)} %get-tuple-element.22) | copy-start | bytes 9437188
  140.7 72.6 %slice-start = ((s8[6291456]{0:T(1024)(128)(4,1)}), s8[2097152]{0:T(1024)(128)(4,1)S(1)}, s32[]{:S(2)}) async-start(s8[6291456]{0:T(1024)(128)(4,1)} %bitcast.128), calls=%async_computation.6 | async-start | bytes 4194304
  197.1 16.3 %slice-start.1 = ((s8[6291456]{0:T(1024)(128)(4,1)}), s8[4194304]{0:T(1024)(128)(4,1)S(1)}, s32[]{:S(2)}) async-start(s8[6291456]{0:T(1024)(128)(4,1)} %bitcast.128), calls=%async_computation.7 | async-start | bytes 8388608
  206.5 6.8 %copy-start.11 = (bf16[8,2,96,384]{3,2,0,1:T(8,128)(2,1)}, bf16[8,2,96,384]{3,2,0,1:T(8,128)(2,1)S(1)}, u32[]{:S(2)}) copy-start(bf16[8,2,96,384]{3,2,0,1:T(8,128)(2,1)S(1)} %get-tuple-element.25) | copy-start | bytes 3538948
  206.6 6.8 %copy-start.7 = (bf16[8,2,96,384]{3,2,0,1:T(8,128)(2,1)}, bf16[8,2,96,384]{3,2,0,1:T(8,128)(2,1)S(1)}, u32[]{:S(2)}) copy-start(bf16[8,2,96,384]{3,2,0,1:T(8,128)(2,1)S(1)} %get-tuple-element.23) | copy-start | bytes 3538948
  206.6 10.0 %copy-start.8 = (bf16[8,2,96,384]{3,2,0,1:T(8,128)(2,1)}, bf16[8,2,96,384]{3,2,0,1:T(8,128)(2,1)S(1)}, u32[]{:S(2)}) copy-start(bf16[8,2,96,384]{3,2,0,1:T(8,128)(2,1)S(1)} %get-tuple-element.24) | copy-start | bytes 3538948
  223.7 1.9 copy-start.6
  233.9 76.3 %all-to-all-start.1 = ((bf16[8,2,96,2048]{3,2,1,0:T(8,128)(2,1)}), bf16[8,2,96,2048]{3,2,1,0:T(8,128)(2,1)}, u32[]{:S(2)}, u32[]{:S(2)}) async-start(bf16[8,2,96,2048]{3,2,1,0:T(8,128)(2,1)} %copy.56), calls=%async_computation.1 | async-start | bytes 12582912 | tf_op jit(solution)/shard_map/all_to_all | solution.py:73
  259.5 55.9 %copy-start.10 = (s32[128,4]{0,1:T(4,128)S(1)}, s32[128,4]{0,1:T(4,128)}, u32[]{:S(2)}) copy-start(s32[128,4]{0,1:T(4,128)} %param.6) | copy-start | bytes 6148
  310.3 76.8 %all-to-all-start.3 = ((bf16[8,2,96,2048]{3,2,1,0:T(8,128)(2,1)}), bf16[8,2,96,2048]{3,2,1,0:T(8,128)(2,1)}, u32[]{:S(2)}, u32[]{:S(2)}) async-start(bf16[8,2,96,2048]{3,2,1,0:T(8,128)(2,1)} %copy.60), calls=%async_computation.3 | async-start | bytes 12582912 | tf_op jit(solution)/shard_map/all_to_all | solution.py:104
  323.7 2.2 copy-start.9
  397.4 5.1 %copy-start.4 = (bf16[128,4,2048]{2,1,0:T(4,128)(2,1)S(1)}, bf16[128,4,2048]{2,1,0:T(4,128)(2,1)}, u32[]{:S(2)}) copy-start(bf16[128,4,2048]{2,1,0:T(4,128)(2,1)} %reshape.163) | copy-start | bytes 6291460
  402.6 11.2 %copy-start.1 = (bf16[128,2048]{1,0:T(8,128)(2,1)S(1)}, bf16[128,2048]{1,0:T(8,128)(2,1)}, u32[]{:S(2)}) copy-start(bf16[128,2048]{1,0:T(8,128)(2,1)} %param.5) | copy-start | bytes 1572868
Sparse Core Ops, SparseCore 0:
  223.9 160.3 reduce-scatter.1
where the time goes:
time: 427 us; the launch traced here: 421 us
  waiting for transfers between devices  158 us (37%)
  local copies, waits for them, and re-layouts  76.2 us (18%)
  blocking collectives  75.2 us (18%)
  matrix products  55.8 us (13%)
  other arithmetic  25.9 us (6%)
  starting transfers between devices  14.9 us (3%)
  between operations  14.5 us (3%)
    all_to_all x1, blocking collectives, forward_pass(): lax.all_to_all(send_rows, 'expert', split_axis=0, concat_axis=0, tiled=True)  75.2 us
    all_to_all x1, waiting for transfers between devices, local(): lax.all_to_all(token_cot, 'expert', split_axis=0, concat_axis=0, tiled=True)  56 us
    all_to_all x1, waiting for transfers between devices, local(): lax.all_to_all(cot_rows, 'expert', split_axis=0, concat_axis=0, tiled=True)  51.6 us
    all_to_all x1, waiting for transfers between devices, forward_pass(): lax.all_to_all(expert_output(hidden, expert_weights), 'expert', split_axi...  50.8 us
    unnamed x31, local copies, waits for them, and re-layouts  10.7 us
    slice x1, local copies, waits for them, and re-layouts, expert_output(): expert_weights[:, 2]  10 us
    mul x2, local copies, waits for them, and re-layouts, local(): gate_probs[:, :, None] * out_grad[:, None, :].astype(jnp.float32)  9.5 us
    dot_general x1, matrix products, expert_backward(): jnp.einsum('sicd,dih->sich', cot_block, expert_weights[:, 2], preferred_e...  9.43 us
  transfers between devices with their start and end apart: 4, of which 3 were waited for; matrix products, arithmetic and copies ran while one was open for 20% of the time, Pallas kernels for 0%

commit v1 on v0

v1 whole, which is shorter than its diff:
```python
import jax
import jax.numpy as jnp
from jax import lax
from jax.sharding import PartitionSpec as P

F32 = jnp.float32
BF16 = jnp.bfloat16


def dot(a, b, ca, cb):
    return lax.dot_general(a, b, (((ca,), (cb,)), ((), ())), preferred_element_type=F32)


def local(tokens, expert_ids, gate_probs, expert_weights, out_grad):
    tok_count, top_count = expert_ids.shape
    d = tokens.shape[1]
    ranks = lax.axis_size("expert")
    me = lax.axis_index("expert")
    local_experts, h = expert_weights.shape[2:]
    n = ranks * tok_count
    eh = local_experts * h

    x = lax.all_gather(tokens, "expert", axis=0, tiled=True)
    small = jnp.concatenate([expert_ids.astype(F32), gate_probs], axis=1)
    small = lax.all_gather(small, "expert", axis=0, tiled=True)
    g = lax.all_gather(out_grad, "expert", axis=0, tiled=True)
    ids = small[:, :top_count].astype(jnp.int32)
    probs = small[:, top_count:]

    mine = me * local_experts + jnp.arange(local_experts, dtype=jnp.int32)
    hit = ids[:, :, None] == mine[None, None, :]
    p = jnp.sum(jnp.where(hit, probs[:, :, None], 0.0), axis=1)

    w = expert_weights.reshape(d, 3 * eh)
    wgu = w[:, : 2 * eh]
    wd = w[:, 2 * eh :]

    a = dot(x, wgu, 1, 0)
    gate = a[:, :eh].reshape(n, local_experts, h)
    up = a[:, eh:].reshape(n, local_experts, h)
    s = jax.nn.sigmoid(gate)
    hidden = gate * s * up
    ph = (p[:, :, None] * hidden).astype(BF16).reshape(n, eh)
    lpart = dot(ph, wd, 1, 1).astype(BF16)
    layer_out = lax.psum_scatter(lpart, "expert", scatter_dimension=0, tiled=True)

    wd_grad = dot(g, ph, 0, 0).astype(BF16)
    wd_grad = lax.psum_scatter(wd_grad, "dp", scatter_dimension=0, tiled=True)

    u = dot(g, wd, 1, 0).reshape(n, local_experts, h)
    gg = jnp.sum(u * hidden, axis=-1)
    hc = p[:, :, None] * u
    gc = (hc * up * s * (1.0 + gate * (1.0 - s))).astype(BF16).reshape(n, eh)
    uc = (hc * gate * s).astype(BF16).reshape(n, eh)
    cots = jnp.concatenate([gc, uc], axis=1)
    tpart = dot(cots, wgu, 1, 1).astype(BF16)
    token_grad = lax.psum_scatter(tpart, "expert", scatter_dimension=0, tiled=True)

    ggk = jnp.sum(jnp.where(hit, gg[:, None, :], 0.0), axis=2)
    gate_grad = lax.psum_scatter(ggk, "expert", scatter_dimension=0, tiled=True)

    wgu_grad = dot(x, cots, 0, 0).astype(BF16)
    wgu_grad = lax.psum_scatter(wgu_grad, "dp", scatter_dimension=0, tiled=True)
    wg = jnp.concatenate([wgu_grad, wd_grad], axis=1)
    weight_grad = wg.astype(F32).reshape(-1, 3, local_experts, h)
    return (layer_out, token_grad, gate_grad, weight_grad)


def solution(mesh):
    tok = P(("expert", "dp"), None)
    wsp = P(None, None, "expert", None)
    return jax.shard_map(
        local,
        mesh=mesh,
        in_specs=(tok, tok, tok, wsp, tok),
        out_specs=(tok, tok, tok, P("dp", None, "expert", None)),
        check_vma=False,
    )
```

time: 427 us -> 439 us (1.028)
  waiting for transfers between devices: 158 us -> 294 us
  blocking collectives: 75.2 us -> 9.09 us
  local copies, waits for them, and re-layouts: 76.2 us -> 56.5 us
  starting transfers between devices: 14.9 us -> 0.46 us
  other arithmetic: 25.9 us -> 12.8 us
  matrix products: 55.8 us -> 49.9 us
    reduce_scatter x1 -> x4, waiting for transfers between devices: 0.01 us -> 269 us  [the longest x1 114 us: local(): wgu_grad = lax.psum_scatter(wgu_grad, 'dp', scatter_dimension=0, tiled=True)]
    all_to_all x3 -> x0, waiting for transfers between devices: 158 us -> none  [the longest x1 56 us: local(): lax.all_to_all(token_cot, 'expert', split_axis=0, concat_axis=0, tiled=True)]
    all_to_all x1 -> x0, blocking collectives: 75.2 us -> none  [forward_pass(): lax.all_to_all(send_rows, 'expert', split_axis=0, concat_axis=0, tiled=True)]
    gather x4 -> x0, local copies, waits for them, and re-layouts: 30.1 us -> none  [the longest x1 8 us: local(): returned.reshape(-1, model_width)[slot_key]]
    reshape x3 -> x4, local copies, waits for them, and re-layouts: 4.65 us -> 28.1 us  [the longest x1 20.9 us: local(): w = expert_weights.reshape(d, 3 * eh)]
    all_gather x0 -> x2, waiting for transfers between devices: none -> 23 us  [the longest x1 13.8 us: local(): g = lax.all_gather(out_grad, 'expert', axis=0, tiled=True)]
    all_to_all x3 -> x0, starting transfers between devices: 14.6 us -> none  [the longest x1 5.17 us: local(): lax.all_to_all(token_cot, 'expert', split_axis=0, concat_axis=0, tiled=True)]
    convert_element_type x2 -> x0, local copies, waits for them, and re-layouts: 9.8 us -> none  [the longest x1 6.61 us: expert_backward(): return (gate_cot, up_cot, token_cot.astype(jnp.bfloat16))]
  transfers between devices with their start and end apart: 4 -> 7, of which waited for: 3 -> 6; matrix products, arithmetic and copies ran while one was open for 20% -> 21% of each run, Pallas kernels for 0% -> 0%
where the time goes in v1:
time: 439 us; the launch traced here: 437 us
  waiting for transfers between devices  294 us (67%)
  local copies, waits for them, and re-layouts  56.5 us (13%)
  matrix products  49.9 us (11%)
  between operations  14.3 us (3%)
  other arithmetic  12.8 us (3%)
  blocking collectives  9.09 us (2%)
    reduce_scatter x1, waiting for transfers between devices, local(): wgu_grad = lax.psum_scatter(wgu_grad, 'dp', scatter_dimension=0, tiled=True)  114 us
    reduce_scatter x1, waiting for transfers between devices, local(): lax.psum_scatter(lpart, 'expert', scatter_dimension=0, tiled=True)  55.3 us
    reduce_scatter x1, waiting for transfers between devices, local(): wd_grad = lax.psum_scatter(wd_grad, 'dp', scatter_dimension=0, tiled=True)  51 us
    dot_general x6, matrix products, dot(): lax.dot_general(a, b, (((ca,), (cb,)), ((), ())), preferred_element_type=...  49.9 us
    reduce_scatter x1, waiting for transfers between devices, local(): lax.psum_scatter(tpart, 'expert', scatter_dimension=0, tiled=True)  49.5 us
    reshape x1, local copies, waits for them, and re-layouts, local(): w = expert_weights.reshape(d, 3 * eh)  20.9 us
    unnamed x22, local copies, waits for them, and re-layouts  15.1 us
    all_gather x1, waiting for transfers between devices, local(): g = lax.all_gather(out_grad, 'expert', axis=0, tiled=True)  13.8 us
  transfers between devices with their start and end apart: 7, of which 6 were waited for; matrix products, arithmetic and copies ran while one was open for 21% of the time, Pallas kernels for 0%

profile of v1, /device:TPU:8, one launch (start us, length us, event | category | flops | bytes accessed | tf_op | source)
XLA Modules:
  0.0 436.8 jit_solution(9271335342334902050)
XLA Ops:
  8.7 20.9 %reshape.38 = bf16[2048,2304]{1,0:T(8,128)(2,1)} reshape(bf16[2048,3,2,384]{3,2,1,0:T(2,128)(2,1)} %param.8) | data formatting | bytes 18874368 | tf_op jit(solution)/shard_map/reshape | solution.py:34
  29.6 9.1 %all_gather.9 = f32[1024,8]{0,1:T(8,128)S(1)} all-gather(f32[128,8]{0,1:T(8,128)S(1)} %pad_maximum_fusion.4), channel_id=1, replica_groups=mesh['expert'=8,'dp'=4] {'expert'}, dimensions={0}, use_global_device_ids=true | all-gather | bytes 36864 | tf_op jit(solution)/shard_map/all_gather | solution.py:25
  38.7 9.1 %all-gather.3.cloned.1.call-done = bf16[1024,2048]{1,0:T(8,128)(2,1)} async-done(((bf16[128,2048]{1,0:T(8,128)(2,1)}), bf16[1024,2048]{1,0:T(8,128)(2,1)}) %all-gather.3.cloned.1.call-update) | async-done | bytes 4194320 | tf_op jit(solution)/shard_map/all_gather | solution.py:23
  47.8 10.0 %fusion.3 = f32[1024,1536]{1,0:T(8,128)S(1)} fusion(bf16[1024,2048]{1,0:T(8,128)(2,1)} %all-gather.3.cloned.1.call-done, bf16[2048,2304]{1,0:T(8,128)(2,1)} %reshape.38), kind=kOutput, calls=%fused_computation.4 | convolution fusion | flops 6442450944 | bytes 16777216 | tf_op jit(solution)/shard_map/dot_general | solution.py:11
  57.9 3.5 fusion.16
  61.4 1.6 copy-done
  63.0 2.4 copy.35
  65.3 2.5 copy.37
  67.8 2.4 copy.38
  70.2 2.5 copy.39
  72.6 13.8 %all-gather.5.cloned.1.call-done = bf16[1024,2048]{1,0:T(8,128)(2,1)} async-done(((bf16[128,2048]{1,0:T(8,128)(2,1)}), bf16[1024,2048]{1,0:T(8,128)(2,1)}) %all-gather.5.cloned.1.call-update) | async-done | bytes 4194320 | tf_op jit(solution)/shard_map/all_gather | solution.py:26
  86.5 6.3 %fusion.9 = f32[1024,768]{0,1:T(8,128)S(1)} fusion(bf16[1024,2048]{1,0:T(8,128)(2,1)} %all-gather.5.cloned.1.call-done, bf16[2048,2304]{1,0:T(8,128)(2,1)} %reshape.38), kind=kOutput, calls=%fused_computation.16 | convolution fusion | flops 3221225472 | bytes 10485760 | tf_op jit(solution)/shard_map/dot_general | solution.py:11
  92.8 2.4 copy.34
  95.2 2.4 copy.40
  97.5 4.8 %multiply_reduce_fusion = f32[1024,2]{0,1:T(2,128)S(1)} fusion(f32[1024,2,384]{2,0,1:T(8,128)} %copy.40, f32[1024,2,384]{2,0,1:T(8,128)} %copy.39, f32[1024,2,384]{2,0,1:T(8,128)} %copy.37), kind=kLoop, calls=%fused_computation.10 | loop fusion | flops 5502976 | bytes 9445376 | tf_op jit(solution)/shard_map/reduce_sum | solution.py:51
  102.7 2.4 mul.62
  105.1 1.9 copy.47
  108.4 6.1 %multiply_convert_fusion.1 = (bf16[1024,768]{1,0:T(8,128)(2,1)}, bf16[1024,768]{1,0:T(8,128)(2,1)}, bf16[1024,768]{1,0:T(8,128)(2,1)S(1)}) fusion(f32[1024,768]{1,0:T(8,128)} %bitcast.22, f32[1024,768]{1,0:T(8,128)S(1)} %copy-done.1, f32[1024,1536]{1,0:T(8,128)} %copy-done), kind=kLoop, calls=%fused_computation.12 | loop fusion | flops 14155776 | bytes 17301504 | tf_op jit(solution)/shard_map/convert_element_type | solution.py:53
  114.4 1.1 copy-done.2
  115.6 4.8 %fusion.8 = bf16[2048,768]{0,1:T(8,128)(2,1)} fusion(bf16[1024,768]{1,0:T(8,128)(2,1)S(1)} %get-tuple-element.32, bf16[1024,2048]{1,0:T(8,128)(2,1)S(1)} %copy-done.8), kind=kOutput, calls=%fused_computation.15 | convolution fusion | flops 3222798336 | bytes 8912896 | tf_op jit(solution)/shard_map/dot_general | solution.py:11
  120.4 1.3 copy-done.4
  122.3 10.9 %fusion = bf16[2048,1536]{0,1:T(8,128)(2,1)} fusion(bf16[1024,2048]{1,0:T(8,128)(2,1)} %all-gather.3.cloned.1.call-done, bf16[1024,768]{1,0:T(8,128)(2,1)S(1)} %copy-done.5, bf16[1024,768]{1,0:T(8,128)(2,1)S(1)} %copy-done.4), kind=kOutput, calls=%fused_computation.1 | convolution fusion | flops 6451888128 | bytes 13631488 | tf_op jit(solution)/shard_map/dot_general | solution.py:11
  133.2 11.0 %fusion.5 = bf16[1024,2048]{1,0:T(8,128)(2,1)} fusion(bf16[2048,2304]{1,0:T(8,128)(2,1)} %reshape.38, bf16[1024,768]{1,0:T(8,128)(2,1)S(1)} %copy-done.5, bf16[1024,768]{1,0:T(8,128)(2,1)S(1)} %copy-done.4), kind=kOutput, calls=%fused_computation.6 | convolution fusion | flops 6450839552 | bytes 13631488 | tf_op jit(solution)/shard_map/dot_general | solution.py:11
  144.3 1.3 copy-done.3
  145.6 6.9 %convolution_convert_fusion.1 = bf16[1024,2048]{1,0:T(8,128)(2,1)} fusion(bf16[1024,768]{1,0:T(8,128)(2,1)S(1)} %copy-done.3, bf16[2048,2304]{1,0:T(8,128)(2,1)} %reshape.38), kind=kOutput, calls=%fused_computation.7 | convolution fusion | flops 3223322624 | bytes 8912896 | tf_op jit(solution)/shard_map/dot_general | solution.py:11
  152.6 1.5 copy.45
  154.1 51.0 %reduce-scatter.14.cloned.1.call-done = bf16[512,768]{0,1:T(8,128)(2,1)} async-done(((bf16[2048,768]{0,1:T(8,128)(2,1)}), bf16[512,768]{0,1:T(8,128)(2,1)}) %reduce-scatter.14.cloned.1.call-update) | async-done | bytes 786448 | tf_op jit(solution)/shard_map/reduce_scatter | solution.py:48
  205.1 113.5 %reduce-scatter.12.cloned.1.call-done = bf16[512,1536]{0,1:T(8,128)(2,1)} async-done(((bf16[2048,1536]{0,1:T(8,128)(2,1)}), bf16[512,1536]{0,1:T(8,128)(2,1)}) %reduce-scatter.12.cloned.1.call-update) | async-done | bytes 1572880 | tf_op jit(solution)/shard_map/reduce_scatter | solution.py:63
  318.6 1.8 pad_maximum_fusion.1
  320.4 4.8 %copy.43 = f32[512,3,2,384]{3,2,1,0:T(2,128)} copy(bf16[512,3,2,384]{0,3,2,1:T(8,128)(2,1)S(1)} %bitcast.23) | data formatting | bytes 7077888
  325.2 49.5 %reduce-scatter.10.cloned.1.call-done = bf16[128,2048]{1,0:T(8,128)(2,1)} async-done(((bf16[1024,2048]{1,0:T(8,128)(2,1)}), bf16[128,2048]{1,0:T(8,128)(2,1)}) %reduce-scatter.10.cloned.1.call-update) | async-done | bytes 524304 | tf_op jit(solution)/shard_map/reduce_scatter | solution.py:57
  374.6 55.3 %reduce-scatter.8.cloned.1.call-done = bf16[128,2048]{1,0:T(8,128)(2,1)} async-done(((bf16[1024,2048]{1,0:T(8,128)(2,1)}), bf16[128,2048]{1,0:T(8,128)(2,1)}) %reduce-scatter.8.cloned.1.call-update) | async-done | bytes 524304 | tf_op jit(solution)/shard_map/reduce_scatter | solution.py:45
  (36 shorter events, 3.9 us)
Async XLA Ops:
  7.2 40.7 %all-gather.3.cloned.1.call-start = ((), (), s32[]{:S(2)}) async-start(), calls=%async_computation.5 | async-start | bytes 4718592 | tf_op jit(solution)/shard_map/all_gather | solution.py:23
  7.9 78.6 %all-gather.5.cloned.1.call-start = ((), (), s32[]{:S(2)}) async-start(), calls=%async_computation.7 | async-start | bytes 4718592 | tf_op jit(solution)/shard_map/all_gather | solution.py:26
  8.6 143.9 %reduce-scatter.16.cloned.1.call-start = ((), (), s32[]{:S(2)}) async-start(), calls=%async_computation.11 | async-start | bytes 589824
  8.7 20.9 %copy-start.6 = (s32[128,4]{0,1:T(4,128)S(1)}, s32[128,4]{0,1:T(4,128)}, u32[]{:S(2)}) copy-start(s32[128,4]{0,1:T(4,128)} %param.6) | copy-start | bytes 6148
  8.7 20.9 %copy-start.7 = (f32[128,4]{0,1:T(4,128)S(1)}, f32[128,4]{0,1:T(4,128)}, u32[]{:S(2)}) copy-start(f32[128,4]{0,1:T(4,128)} %param.7) | copy-start | bytes 6148
  57.9 5.1 %copy-start = (f32[1024,1536]{1,0:T(8,128)}, f32[1024,1536]{1,0:T(8,128)S(1)}, u32[]{:S(2)}) copy-start(f32[1024,1536]{1,0:T(8,128)S(1)} %fusion.3) | copy-start | bytes 18874372
  105.1 3.2 copy-start.1
  108.1 96.9 %reduce-scatter.14.cloned.1.call-start = ((), (), s32[]{:S(2)}) async-start(), calls=%async_computation.10 | async-start | bytes 3932160 | tf_op jit(solution)/shard_map/reduce_scatter | solution.py:48
  108.3 7.2 %copy-start.8 = (bf16[1024,2048]{1,0:T(8,128)(2,1)S(1)}, bf16[1024,2048]{1,0:T(8,128)(2,1)}, u32[]{:S(2)}) copy-start(bf16[1024,2048]{1,0:T(8,128)(2,1)} %all-gather.5.cloned.1.call-done) | copy-start | bytes 12582916
  114.4 1.1 copy-start.2
  120.4 1.4 copy-start.4
  120.4 1.9 copy-start.5
  120.4 198.2 %reduce-scatter.12.cloned.1.call-start = ((), (), s32[]{:S(2)}) async-start(), calls=%async_computation.9 | async-start | bytes 7864320 | tf_op jit(solution)/shard_map/reduce_scatter | solution.py:63
  133.2 241.5 %reduce-scatter.10.cloned.1.call-start = ((), (), s32[]{:S(2)}) async-start(), calls=%async_computation.8 | async-start | bytes 4718592 | tf_op jit(solution)/shard_map/reduce_scatter | solution.py:57
  144.2 1.4 copy-start.3
  144.3 285.7 %reduce-scatter.8.cloned.1.call-start = ((), (), s32[]{:S(2)}) async-start(), calls=%async_computation.6 | async-start | bytes 4718592 | tf_op jit(solution)/shard_map/reduce_scatter | solution.py:45
Sparse Core Ops, SparseCore 0:
  9.9 37.9 all-gather.2
  49.7 36.6 all-gather.4
  108.2 34.1 reduce-scatter.15
  145.2 59.7 reduce-scatter.13
  207.3 111.2 reduce-scatter.11
  322.7 51.8 reduce-scatter.9
  378.6 51.3 reduce-scatter.7

commit v2 on v1

v2 whole, which is shorter than its diff:
```python
import jax
import jax.numpy as jnp
from jax import lax
from jax.sharding import Mesh, PartitionSpec as P

F32 = jnp.float32
BF16 = jnp.bfloat16
SWAP = [(0, 1), (1, 0)]


def dot(a, b, ca, cb):
    return lax.dot_general(a, b, (((ca,), (cb,)), ((), ())), preferred_element_type=F32)


def gather(rows):
    own = lax.all_gather(rows, "chip", axis=0, tiled=True)
    return own, lax.ppermute(own, "core", SWAP)


def scatter(own, other):
    total = own + lax.ppermute(other, "core", SWAP).astype(F32)
    return lax.psum_scatter(
        total.astype(other.dtype), "chip", scatter_dimension=0, tiled=True
    )


def line_scatter(grad):
    n = lax.axis_size("dp")
    me = lax.axis_index("dp")
    rows = grad.shape[0] // n

    def chunk(i):
        i = jnp.clip(i, 0, n - 1)
        return lax.dynamic_slice_in_dim(grad, i * rows, rows, 0).astype(F32)

    up = down = None
    for t in range(n - 1):
        a = chunk(n - 1 - t + me)
        b = chunk(t - (n - 1) + me)
        if t:
            a = a + up.astype(F32)
            b = b + down.astype(F32)
        up = lax.ppermute(a.astype(BF16), "dp", [(i, i + 1) for i in range(t + 1)])
        down = lax.ppermute(
            b.astype(BF16), "dp", [(i, i - 1) for i in range(n - 1 - t, n)]
        )
    return chunk(me) + up.astype(F32) + down.astype(F32)


def local(tokens, expert_ids, gate_probs, expert_weights, out_grad):
    tok_count, top_count = expert_ids.shape
    d = tokens.shape[1]
    chips = lax.axis_size("chip")
    core = lax.axis_index("core")
    me = lax.axis_index("chip") * 2 + core
    local_experts, h = expert_weights.shape[2:]
    half = chips * tok_count
    eh = local_experts * h

    x = jnp.concatenate(gather(tokens), axis=0)
    g = jnp.concatenate(gather(out_grad), axis=0)
    small = jnp.concatenate([expert_ids.astype(F32), gate_probs], axis=1)
    small = lax.all_gather(small, ("chip", "core"), axis=0)
    small = small.reshape(chips, 2, tok_count, 2 * top_count)
    small = jnp.where(core == 0, small, small[:, ::-1])
    small = small.transpose(1, 0, 2, 3).reshape(2 * half, 2 * top_count)
    ids = small[:, :top_count].astype(jnp.int32)
    probs = small[:, top_count:]

    hits = [ids == me * local_experts + i for i in range(local_experts)]
    p = jnp.concatenate(
        [
            jnp.broadcast_to(
                jnp.sum(jnp.where(hit, probs, 0.0), axis=1, keepdims=True), (2 * half, h)
            )
            for hit in hits
        ],
        axis=1,
    )

    w = expert_weights.reshape(d, 3 * eh)
    wgu = w[:, : 2 * eh]
    wd = w[:, 2 * eh :]

    a = dot(x, wgu, 1, 0)
    gate = a[:, :eh]
    up = a[:, eh:]
    s = jax.nn.sigmoid(gate)
    hidden = gate * s * up
    ph = (p * hidden).astype(BF16)
    down_grad = line_scatter(dot(g, ph, 0, 0).astype(BF16))

    u = dot(g, wd, 1, 0)
    hc = p * u
    gc = (hc * up * s * (1.0 + gate * (1.0 - s))).astype(BF16)
    uc = (hc * gate * s).astype(BF16)
    gate_part = line_scatter(dot(x, gc, 0, 0).astype(BF16))
    up_part = line_scatter(dot(x, uc, 0, 0).astype(BF16))

    other = dot(ph[half:], wd, 1, 1).astype(BF16)
    layer_out = scatter(dot(ph[:half], wd, 1, 1), other)

    cots = jnp.concatenate([gc, uc], axis=1)
    other = dot(cots[half:], wgu, 1, 1).astype(BF16)
    token_grad = scatter(dot(cots[:half], wgu, 1, 1), other)

    uh = u * hidden
    ggk = sum(
        jnp.where(hit, jnp.sum(uh[:, i * h : (i + 1) * h], axis=1, keepdims=True), 0.0)
        for i, hit in enumerate(hits)
    )
    gate_grad = scatter(ggk[:half], ggk[half:])

    weight_grad = jnp.stack([gate_part, up_part, down_grad], axis=1)
    weight_grad = weight_grad.reshape(-1, 3, local_experts, h)
    return (layer_out, token_grad, gate_grad, weight_grad)


def solution(mesh):
    experts, groups = mesh.devices.shape
    split = Mesh(
        mesh.devices.reshape(experts // 2, 2, groups), ("chip", "core", "dp")
    )
    tok = P(("chip", "core", "dp"), None)
    wsp = P(None, None, ("chip", "core"), None)
    return jax.shard_map(
        local,
        mesh=split,
        in_specs=(tok, tok, tok, wsp, tok),
        out_specs=(tok, tok, tok, P("dp", None, ("chip", "core"), None)),
        check_vma=False,
    )
```

time: 439 us -> 324 us (0.74)
  waiting for transfers between devices: 294 us -> 131 us
  starting transfers between devices: 0.46 us -> 40.5 us
  other arithmetic: 12.8 us -> 41.7 us
  local copies, waits for them, and re-layouts: 56.5 us -> 41.5 us
  matrix products: 49.9 us -> 44.5 us
    reduce_scatter x4 -> x2, waiting for transfers between devices: 269 us -> 0.01 us  [scatter(): lax.psum_scatter(total.astype(other.dtype), 'chip', scatter_dimension=0,...]
    ppermute x0 -> x23, waiting for transfers between devices: none -> 85.4 us  [the longest x9 55.2 us: line_scatter(): up = lax.ppermute(a.astype(BF16), 'dp', [(i, i + 1) for i in range(t + 1)])]
    ppermute x0 -> x23, starting transfers between devices: none -> 40.3 us  [the longest x9 20.1 us: line_scatter(): up = lax.ppermute(a.astype(BF16), 'dp', [(i, i + 1) for i in range(t + 1)])]
    all_gather x2, waiting for transfers between devices: 23 us -> 43.6 us  [gather(): own = lax.all_gather(rows, 'chip', axis=0, tiled=True)]
    convert_element_type x1 -> x10, other arithmetic: 6.05 us -> 25.2 us  [the longest x6 14.4 us: line_scatter(): up = lax.ppermute(a.astype(BF16), 'dp', [(i, i + 1) for i in range(t + 1)])]
    unnamed x22 -> x34, local copies, waits for them, and re-layouts: 15.1 us -> 5.24 us
    another operation x0 -> x3, local copies, waits for them, and re-layouts: none -> 9.22 us  [local(): weight_grad = jnp.stack([gate_part, up_part, down_grad], axis=1)]
    add x1 -> x5, other arithmetic: 0.01 us -> 9.09 us  [the longest x3 9.06 us: line_scatter(): return chunk(me) + up.astype(F32) + down.astype(F32)]
  transfers between devices with their start and end apart: 7 -> 28, of which waited for: 6 -> 11; matrix products, arithmetic and copies ran while one was open for 21% -> 36% of each run, Pallas kernels for 0% -> 0%
where the time goes in v2:
time: 324 us; the launch traced here: 322 us
  waiting for transfers between devices  131 us (40%)
  matrix products  44.5 us (14%)
  other arithmetic  41.7 us (13%)
  local copies, waits for them, and re-layouts  41.5 us (13%)
  starting transfers between devices  40.5 us (12%)
  between operations  14.3 us (4%)
  blocking collectives  9 us (3%)
    ppermute x9, waiting for transfers between devices, line_scatter(): up = lax.ppermute(a.astype(BF16), 'dp', [(i, i + 1) for i in range(t + 1)])  55.2 us
    dot_general x9, matrix products, dot(): lax.dot_general(a, b, (((ca,), (cb,)), ((), ())), preferred_element_type=...  44.5 us
    all_gather x2, waiting for transfers between devices, gather(): own = lax.all_gather(rows, 'chip', axis=0, tiled=True)  43.6 us
    ppermute x9, waiting for transfers between devices, line_scatter(): lax.ppermute(b.astype(BF16), 'dp', [(i, i - 1) for i in range(n - 1 - t,...  30.3 us
    reshape x1, local copies, waits for them, and re-layouts, local(): w = expert_weights.reshape(d, 3 * eh)  20.8 us
    ppermute x9, starting transfers between devices, line_scatter(): up = lax.ppermute(a.astype(BF16), 'dp', [(i, i + 1) for i in range(t + 1)])  20.1 us
    ppermute x9, starting transfers between devices, line_scatter(): lax.ppermute(b.astype(BF16), 'dp', [(i, i - 1) for i in range(n - 1 - t,...  19.1 us
    convert_element_type x6, other arithmetic, line_scatter(): up = lax.ppermute(a.astype(BF16), 'dp', [(i, i + 1) for i in range(t + 1)])  14.4 us
  transfers between devices with their start and end apart: 28, of which 11 were waited for; matrix products, arithmetic and copies ran while one was open for 36% of the time, Pallas kernels for 0%

profile of v2, /device:TPU:8, one launch (start us, length us, event | category | flops | bytes accessed | tf_op | source)
XLA Modules:
  0.0 322.1 jit_solution(12631670777283174412)
XLA Ops:
  8.7 37.7 %all-gather.4.cloned.1.call-done = bf16[512,2048]{1,0:T(8,128)(2,1)} async-done(((bf16[128,2048]{1,0:T(8,128)(2,1)}), bf16[512,2048]{1,0:T(8,128)(2,1)}) %all-gather.4.cloned.1.call-update) | async-done | bytes 2097168 | tf_op jit(solution)/shard_map/all_gather | solution.py:16
  47.7 9.0 %all-gather = f32[1024,8]{0,1:T(8,128)S(1)} all-gather(f32[128,8]{0,1:T(8,128)S(1)} %pad_maximum_fusion.4), channel_id=2, replica_groups=mesh['chip'=4,'core'=2,'dp'=4] {'chip','core'}, dimensions={0}, use_global_device_ids=true | all-gather | bytes 36864 | tf_op jit(solution)/shard_map/all_gather | solution.py:63
  56.7 20.8 %reshape.30 = bf16[2048,2304]{1,0:T(8,128)(2,1)} reshape(bf16[2048,3,2,384]{3,2,1,0:T(2,128)(2,1)} %param.8) | data formatting | bytes 18874368 | tf_op jit(solution)/shard_map/reshape | solution.py:81
  77.6 6.0 %all-gather.6.cloned.1.call-done = bf16[512,2048]{1,0:T(8,128)(2,1)} async-done(((bf16[128,2048]{1,0:T(8,128)(2,1)}), bf16[512,2048]{1,0:T(8,128)(2,1)}) %all-gather.6.cloned.1.call-update) | async-done | bytes 2097168 | tf_op jit(solution)/shard_map/all_gather | solution.py:16
  88.5 6.7 %fusion.4 = f32[1024,1536]{1,0:T(8,128)S(1)} fusion(bf16[1024,2048]{1,0:T(8,128)(2,1)S(1)} %constant_dynamic-update-slice_fusion, bf16[2048,2304]{1,0:T(8,128)(2,1)S(1)} %copy-done.4), kind=kOutput, calls=%fused_computation.4 | convolution fusion | flops 6442450944 | bytes 16777216 | tf_op jit(solution)/shard_map/dot_general | solution.py:12
  95.4 3.8 %fusion.32 = (f32[1024,768]{1,0:T(8,128)S(1)}, f32[1024,768]{1,0:T(8,128)S(1)}) fusion(f32[1024,1536]{1,0:T(8,128)S(1)} %fusion.4, bf16[1024,2048]{1,0:T(8,128)(2,1)S(1)} %constant_dynamic-update-slice_fusion.2, bf16[2048,2304]{1,0:T(8,128)(2,1)S(1)} %copy-done.4), kind=kOutput, calls=%fused_computation.72 | convolution fusion | flops 3225944064 | bytes 19922944 | tf_op jit(solution)/shard_map/dot_general | solution.py:12
  100.0 3.5 %multiply_convert_fusion.1 = (bf16[1024,768]{1,0:T(8,128)(2,1)}, bf16[1024,768]{1,0:T(8,128)(2,1)}, bf16[1024,768]{1,0:T(8,128)(2,1)S(1)}) fusion(f32[1024,1536]{1,0:T(8,128)S(1)} %fusion.4, f32[1024,768]{1,0:T(8,128)S(1)} %get-tuple-element.27, f32[1024,384]{1,0:T(8,128)S(1)} %broadcast_in_dim.37, f32[1024,384]{1,0:T(8,128)S(1)} %broadcast_in_dim.36), kind=kLoop, calls=%fused_computation.19 | loop fusion | flops 14942208 | bytes 17301504 | tf_op jit(solution)/shard_map/convert_element_type | solution.py:95
  103.5 3.2 convolution_convert_fusion.3
  107.3 6.1 %convolution_convert_fusion = bf16[2048,768]{0,1:T(8,128)(2,1)S(1)} fusion(bf16[1024,2048]{1,0:T(8,128)(2,1)} %copy-done.9, bf16[1024,768]{1,0:T(8,128)(2,1)} %copy-done.8), kind=kOutput, calls=%fused_computation.9 | convolution fusion | flops 3222798336 | bytes 8912896 | tf_op jit(solution)/shard_map/dot_general | solution.py:12
  114.4 6.0 %add_convert_fusion.1 = bf16[512,2048]{1,0:T(8,128)(2,1)} fusion(bf16[512,2048]{1,0:T(8,128)(2,1)} %collective-permute-done.1, bf16[2048,2304]{1,0:T(8,128)(2,1)} %reshape.30, bf16[1024,768]{1,0:T(8,128)(2,1)} %copy-done.8), kind=kOutput, calls=%fused_computation.8 | convolution fusion | flops 1613758464 | bytes 8126464 | tf_op jit(solution)/shard_map/dot_general | solution.py:12
  123.0 6.7 %fusion.9 = bf16[512,2048]{1,0:T(8,128)(2,1)S(1)} fusion(bf16[2048,2304]{1,0:T(8,128)(2,1)} %reshape.30, bf16[1024,768]{1,0:T(8,128)(2,1)S(1)} %copy-done.7, bf16[1024,768]{1,0:T(8,128)(2,1)S(1)} %copy-done.6), kind=kOutput, calls=%fused_computation.22 | convolution fusion | flops 3225419776 | bytes 11534336 | tf_op jit(solution)/shard_map/dot_general | solution.py:12
  130.2 3.7 %convolution_convert_fusion.2 = bf16[2048,768]{0,1:T(8,128)(2,1)S(1)} fusion(bf16[1024,2048]{1,0:T(8,128)(2,1)S(1)} %copy-done.11, bf16[1024,768]{1,0:T(8,128)(2,1)S(1)} %copy-done.6), kind=kOutput, calls=%fused_computation.11 | convolution fusion | flops 3222798336 | bytes 8912896 | tf_op jit(solution)/shard_map/dot_general | solution.py:12
  136.6 3.7 %convolution_convert_fusion.1 = bf16[2048,768]{0,1:T(8,128)(2,1)S(1)} fusion(bf16[1024,2048]{1,0:T(8,128)(2,1)S(1)} %copy-done.11, bf16[1024,768]{1,0:T(8,128)(2,1)S(1)} %copy-done.7), kind=kOutput, calls=%fused_computation.10 | convolution fusion | flops 3222798336 | bytes 8912896 | tf_op jit(solution)/shard_map/dot_general | solution.py:12
  147.7 13.1 %collective-permute-done.5 = bf16[512,768]{0,1:T(8,128)(2,1)S(1)} collective-permute-done((bf16[512,768]{0,1:T(8,128)(2,1)S(1)}, bf16[512,768]{0,1:T(8,128)(2,1)S(1)}, u32[]{:S(2)}, u32[]{:S(2)}) %collective-permute-start.5) | collective-permute-done | bytes 786464 | tf_op jit(solution)/shard_map/ppermute | solution.py:43
  165.8 4.7 %add_convert_fusion = bf16[512,2048]{1,0:T(8,128)(2,1)} fusion(bf16[512,2048]{1,0:T(8,128)(2,1)S(1)} %collective-permute-done.3, bf16[2048,2304]{1,0:T(8,128)(2,1)S(1)} %bitcast.17, bf16[1024,768]{1,0:T(8,128)(2,1)S(1)} %copy-done.6, bf16[1024,768]{1,0:T(8,128)(2,1)S(1)} %copy-done.7), kind=kOutput, calls=%fused_computation.7 | convolution fusion | flops 3227516928 | bytes 13631488 | tf_op jit(solution)/shard_map/dot_general | solution.py:12
  170.5 7.2 %collective-permute-done.11 = bf16[512,768]{0,1:T(8,128)(2,1)} collective-permute-done((bf16[512,768]{0,1:T(8,128)(2,1)}, bf16[512,768]{0,1:T(8,128)(2,1)}, u32[]{:S(2)}, u32[]{:S(2)}) %collective-permute-start.11) | collective-permute-done | bytes 786464 | tf_op jit(solution)/shard_map/ppermute | solution.py:43
  183.6 10.9 %collective-permute-done.18 = bf16[512,768]{0,1:T(8,128)(2,1)} collective-permute-done((bf16[512,768]{0,1:T(8,128)(2,1)}, bf16[512,768]{0,1:T(8,128)(2,1)}, u32[]{:S(2)}, u32[]{:S(2)}) %collective-permute-start.18) | collective-permute-done | bytes 786464 | tf_op jit(solution)/shard_map/ppermute | solution.py:43
  194.6 3.2 %add_convert_fusion.4 = (bf16[512,768]{0,1:T(8,128)(2,1)}, bf16[512,768]{0,1:T(8,128)(2,1)}) fusion(bf16[512,768]{0,1:T(8,128)(2,1)} %collective-permute-done.18, bf16[2048,768]{0,1:T(8,128)(2,1)S(1)} %convolution_convert_fusion, s32[]{:T(128)S(6)} %select_n.64, bf16[512,768]{0,1:T(8,128)(2,1)} %collective-permute-done.20, s32[]{:T(128)S(6)} %select_n.68), kind=kLoop, calls=%fused_computation.37 | loop fusion | flops 3145728 | bytes 4718600 | tf_op jit(solution)/shard_map/convert_element_type | solution.py:43
  199.4 12.0 %collective-permute-done.6 = bf16[512,768]{0,1:T(8,128)(2,1)} collective-permute-done((bf16[512,768]{0,1:T(8,128)(2,1)}, bf16[512,768]{0,1:T(8,128)(2,1)}, u32[]{:S(2)}, u32[]{:S(2)}) %collective-permute-start.6) | collective-permute-done | bytes 786464 | tf_op jit(solution)/shard_map/ppermute | solution.py:43
  211.4 3.2 add_convert_fusion.12
  215.9 11.9 %collective-permute-done.12 = bf16[512,768]{0,1:T(8,128)(2,1)} collective-permute-done((bf16[512,768]{0,1:T(8,128)(2,1)}, bf16[512,768]{0,1:T(8,128)(2,1)}, u32[]{:S(2)}, u32[]{:S(2)}) %collective-permute-start.12) | collective-permute-done | bytes 786464 | tf_op jit(solution)/shard_map/ppermute | solution.py:43
  227.8 3.2 add_convert_fusion.8
  232.3 4.6 %collective-permute-start.19 = (bf16[512,768]{0,1:T(8,128)(2,1)}, bf16[512,768]{0,1:T(8,128)(2,1)}, u32[]{:S(2)}, u32[]{:S(2)}) collective-permute-start(bf16[512,768]{0,1:T(8,128)(2,1)} %get-tuple-element.22), channel_id=1, source_target_pairs={{0,1},{1,2},{2,3},{4,5},{5,6},{6,7},{8,9},{9,10},{10,11},{12,13},{... | collective-permute-start | bytes 2359304 | tf_op jit(solution)/shard_map/ppermute | solution.py:43
  241.3 3.7 %collective-permute-start.7 = (bf16[512,768]{0,1:T(8,128)(2,1)}, bf16[512,768]{0,1:T(8,128)(2,1)}, u32[]{:S(2)}, u32[]{:S(2)}) collective-permute-start(bf16[512,768]{0,1:T(8,128)(2,1)} %get-tuple-element.14), channel_id=1, source_target_pairs={{0,1},{1,2},{2,3},{4,5},{5,6},{6,7},{8,9},{9,10},{10,11},{12,13},{... | collective-permute-start | bytes 2359304 | tf_op jit(solution)/shard_map/ppermute | solution.py:43
  250.5 3.1 collective-permute-done.15
  258.1 4.8 %collective-permute-start.16 = (bf16[512,768]{0,1:T(8,128)(2,1)}, bf16[512,768]{0,1:T(8,128)(2,1)}, u32[]{:S(2)}, u32[]{:S(2)}) collective-permute-start(bf16[512,768]{0,1:T(8,128)(2,1)} %add_convert_fusion.6), channel_id=1, source_target_pairs={{1,0},{2,1},{3,2},{5,4},{6,5},{7,6},{9,8},{10,9},{11,10},{13,12},{... | collective-permute-start | bytes 2359304 | tf_op jit(solution)/shard_map/ppermute | solution.py:44
  264.4 6.1 %collective-permute-done.22 = bf16[512,768]{0,1:T(8,128)(2,1)} collective-permute-done((bf16[512,768]{0,1:T(8,128)(2,1)}, bf16[512,768]{0,1:T(8,128)(2,1)}, u32[]{:S(2)}, u32[]{:S(2)}) %collective-permute-start.22) | collective-permute-done | bytes 786464 | tf_op jit(solution)/shard_map/ppermute | solution.py:44
  276.2 11.2 %collective-permute-done.10 = bf16[512,768]{0,1:T(8,128)(2,1)} collective-permute-done((bf16[512,768]{0,1:T(8,128)(2,1)}, bf16[512,768]{0,1:T(8,128)(2,1)}, u32[]{:S(2)}, u32[]{:S(2)}) %collective-permute-start.10) | collective-permute-done | bytes 786464 | tf_op jit(solution)/shard_map/ppermute | solution.py:44
  287.4 3.1 convert_add_fusion.2
  293.2 9.9 %collective-permute-done.16 = bf16[512,768]{0,1:T(8,128)(2,1)} collective-permute-done((bf16[512,768]{0,1:T(8,128)(2,1)}, bf16[512,768]{0,1:T(8,128)(2,1)}, u32[]{:S(2)}, u32[]{:S(2)}) %collective-permute-start.16) | collective-permute-done | bytes 786464 | tf_op jit(solution)/shard_map/ppermute | solution.py:44
  306.2 3.7 %copy.21 = f32[512,1,2,384]{3,2,1,0:T(2,128)} copy(f32[512,1,2,384]{0,3,2,1:T(8,128)} %bitcast.18) | data formatting | bytes 3145728 | tf_op jit(solution)/shard_map/stack | solution.py:114
  309.9 5.7 %pad_maximum_fusion = f32[512,3,2,384]{3,2,1,0:T(2,128)} fusion(f32[512,1,2,384]{3,2,1,0:T(2,128)S(1)} %copy.22, f32[512,1,2,384]{3,2,1,0:T(2,128)} %copy.21, f32[512,1,2,384]{3,2,1,0:T(2,128)S(1)} %copy.20), kind=kLoop, calls=%fused_computation.6 | loop fusion | flops 2359296 | bytes 9437184 | tf_op jit(solution)/shard_map/stack | solution.py:114
  (108 shorter events, 65.8 us)
Async XLA Ops:
  7.2 39.2 %all-gather.4.cloned.1.call-start = ((), (), s32[]{:S(2)}) async-start(), calls=%async_computation.3 | async-start | bytes 2621440 | tf_op jit(solution)/shard_map/all_gather | solution.py:16
  7.9 75.6 %all-gather.6.cloned.1.call-start = ((), (), s32[]{:S(2)}) async-start(), calls=%async_computation.5 | async-start | bytes 2621440 | tf_op jit(solution)/shard_map/all_gather | solution.py:16
  8.6 254.3 %reduce-scatter.10.cloned.1.call-start = ((), (), s32[]{:S(2)}) async-start(), calls=%async_computation.7 | async-start | bytes 327680
  46.4 39.2 %collective-permute-start = (bf16[512,2048]{1,0:T(8,128)(2,1)}, bf16[512,2048]{1,0:T(8,128)(2,1)}, u32[]{:S(2)}, u32[]{:S(2)}) collective-permute-start(bf16[512,2048]{1,0:T(8,128)(2,1)} %all-gather.4.cloned.1.call-done), channel_id=1, source_target_pairs={{0,4},{4,0},{1,5},{5,1},{2,6},{6,2},{3,7},{7,3},{8,12},{12,8},{9,1... | collective-permute-start | bytes 6291464 | tf_op jit(solution)/shard_map/ppermute | solution.py:17
  83.5 11.6 %collective-permute-start.2 = (bf16[512,2048]{1,0:T(8,128)(2,1)}, bf16[512,2048]{1,0:T(8,128)(2,1)S(1)}, u32[]{:S(2)}, u32[]{:S(2)}) collective-permute-start(bf16[512,2048]{1,0:T(8,128)(2,1)} %all-gather.6.cloned.1.call-done), channel_id=1, source_target_pairs={{0,4},{4,0},{1,5},{5,1},{2,6},{6,2},{3,7},{7,3},{8,12},{12,8},{9,1... | collective-permute-start | bytes 6291464 | tf_op jit(solution)/shard_map/ppermute | solution.py:17
  106.7 7.7 %collective-permute-start.1 = (bf16[512,2048]{1,0:T(8,128)(2,1)}, bf16[512,2048]{1,0:T(8,128)(2,1)}, u32[]{:S(2)}, u32[]{:S(2)}) collective-permute-start(bf16[512,2048]{1,0:T(8,128)(2,1)} %convolution_convert_fusion.3), channel_id=1, source_target_pairs={{0,4},{4,0},{1,5},{5,1},{2,6},{6,2},{3,7},{7,3},{8,12},{12,8},{9,1... | collective-permute-start | bytes 6291464 | tf_op jit(solution)/shard_map/ppermute | solution.py:21
  107.2 6.2 %collective-permute-start.4 = (f32[512,4]{0,1:T(4,128)S(1)}, f32[512,4]{0,1:T(4,128)S(1)}, u32[]{:S(2)}, u32[]{:S(2)}) collective-permute-start(f32[512,4]{0,1:T(4,128)S(1)} %slice.69), channel_id=1, source_target_pairs={{0,4},{4,0},{1,5},{5,1},{2,6},{6,2},{3,7},{7,3},{8,12},{12,8},{9,1... | collective-permute-start | bytes 24584 | tf_op jit(solution)/shard_map/ppermute | solution.py:21
  114.3 201.2 %reduce-scatter.6.cloned.1.call-start = ((), (), s32[]{:S(2)}) async-start(), calls=%async_computation.4 | async-start | bytes 2621440 | tf_op jit(solution)/shard_map/reduce_scatter | solution.py:22
  120.4 195.2 %reduce-scatter.8.cloned.1.call-start = ((), (), s32[]{:S(2)}) async-start(), calls=%async_computation.6 | async-start | bytes 2621440 | tf_op jit(solution)/shard_map/reduce_scatter | solution.py:22
  121.5 23.6 %collective-permute-start.17 = (bf16[512,768]{0,1:T(8,128)(2,1)S(1)}, bf16[512,768]{0,1:T(8,128)(2,1)S(1)}, u32[]{:S(2)}, u32[]{:S(2)}) collective-permute-start(bf16[512,768]{0,1:T(8,128)(2,1)S(1)} %get-tuple-element.24), channel_id=1, source_target_pairs={{0,1},{4,5},{8,9},{12,13},{16,17},{20,21},{24,25},{28,29}} | collective-permute-start | bytes 2359304 | tf_op jit(solution)/shard_map/ppermute | solution.py:43
  129.7 34.2 %collective-permute-start.3 = (bf16[512,2048]{1,0:T(8,128)(2,1)S(1)}, bf16[512,2048]{1,0:T(8,128)(2,1)S(1)}, u32[]{:S(2)}, u32[]{:S(2)}) collective-permute-start(bf16[512,2048]{1,0:T(8,128)(2,1)S(1)} %fusion.9), channel_id=1, source_target_pairs={{0,4},{4,0},{1,5},{5,1},{2,6},{6,2},{3,7},{7,3},{8,12},{12,8},{9,1... | collective-permute-start | bytes 6291464 | tf_op jit(solution)/shard_map/ppermute | solution.py:21
  133.9 31.8 %slice-start = ((s8[9437184]{0:T(1024)(128)(4,1)}), s8[4194304]{0:T(1024)(128)(4,1)S(1)}, s32[]{:S(2)}) async-start(s8[9437184]{0:T(1024)(128)(4,1)} %bitcast.16), calls=%async_computation.8 | async-start | bytes 8388608
  135.0 30.7 %slice-start.1 = ((s8[9437184]{0:T(1024)(128)(4,1)}), s8[4194304]{0:T(1024)(128)(4,1)S(1)}, s32[]{:S(2)}) async-start(s8[9437184]{0:T(1024)(128)(4,1)} %bitcast.16), calls=%async_computation.9 | async-start | bytes 8388608
  135.0 30.7 %slice-start.2 = ((s8[9437184]{0:T(1024)(128)(4,1)}), s8[1048576]{0:T(1024)(128)(4,1)S(1)}, s32[]{:S(2)}) async-start(s8[9437184]{0:T(1024)(128)(4,1)} %bitcast.16), calls=%async_computation.10 | async-start | bytes 2097152
  135.0 25.7 %collective-permute-start.5 = (bf16[512,768]{0,1:T(8,128)(2,1)S(1)}, bf16[512,768]{0,1:T(8,128)(2,1)S(1)}, u32[]{:S(2)}, u32[]{:S(2)}) collective-permute-start(bf16[512,768]{0,1:T(8,128)(2,1)S(1)} %get-tuple-element.16), channel_id=1, source_target_pairs={{0,1},{4,5},{8,9},{12,13},{16,17},{20,21},{24,25},{28,29}} | collective-permute-start | bytes 2359304 | tf_op jit(solution)/shard_map/ppermute | solution.py:43
  140.4 41.3 %collective-permute-start.20 = (bf16[512,768]{0,1:T(8,128)(2,1)}, bf16[512,768]{0,1:T(8,128)(2,1)}, u32[]{:S(2)}, u32[]{:S(2)}) collective-permute-start(bf16[512,768]{0,1:T(8,128)(2,1)} %get-tuple-element.25), channel_id=1, source_target_pairs={{3,2},{7,6},{11,10},{15,14},{19,18},{23,22},{27,26},{31,30}} | collective-permute-start | bytes 2359304 | tf_op jit(solution)/shard_map/ppermute | solution.py:44
  142.3 57.1 %collective-permute-start.8 = (bf16[512,768]{0,1:T(8,128)(2,1)}, bf16[512,768]{0,1:T(8,128)(2,1)}, u32[]{:S(2)}, u32[]{:S(2)}) collective-permute-start(bf16[512,768]{0,1:T(8,128)(2,1)} %get-tuple-element.17), channel_id=1, source_target_pairs={{3,2},{7,6},{11,10},{15,14},{19,18},{23,22},{27,26},{31,30}} | collective-permute-start | bytes 2359304 | tf_op jit(solution)/shard_map/ppermute | solution.py:44
  145.2 32.5 %collective-permute-start.11 = (bf16[512,768]{0,1:T(8,128)(2,1)}, bf16[512,768]{0,1:T(8,128)(2,1)}, u32[]{:S(2)}, u32[]{:S(2)}) collective-permute-start(bf16[512,768]{0,1:T(8,128)(2,1)} %get-tuple-element.20), channel_id=1, source_target_pairs={{0,1},{4,5},{8,9},{12,13},{16,17},{20,21},{24,25},{28,29}} | collective-permute-start | bytes 2359304 | tf_op jit(solution)/shard_map/ppermute | solution.py:43
  160.7 33.8 %collective-permute-start.18 = (bf16[512,768]{0,1:T(8,128)(2,1)}, bf16[512,768]{0,1:T(8,128)(2,1)}, u32[]{:S(2)}, u32[]{:S(2)}) collective-permute-start(bf16[512,768]{0,1:T(8,128)(2,1)} %add_convert_fusion.5), channel_id=1, source_target_pairs={{0,1},{1,2},{4,5},{5,6},{8,9},{9,10},{12,13},{13,14},{16,17},{17,1... | collective-permute-start | bytes 2359304 | tf_op jit(solution)/shard_map/ppermute | solution.py:43
  163.8 47.6 %collective-permute-start.6 = (bf16[512,768]{0,1:T(8,128)(2,1)}, bf16[512,768]{0,1:T(8,128)(2,1)}, u32[]{:S(2)}, u32[]{:S(2)}) collective-permute-start(bf16[512,768]{0,1:T(8,128)(2,1)} %add_convert_fusion.13), channel_id=1, source_target_pairs={{0,1},{1,2},{4,5},{5,6},{8,9},{9,10},{12,13},{13,14},{16,17},{17,1... | collective-permute-start | bytes 2359304 | tf_op jit(solution)/shard_map/ppermute | solution.py:43
  177.7 38.2 %collective-permute-start.14 = (bf16[512,768]{0,1:T(8,128)(2,1)}, bf16[512,768]{0,1:T(8,128)(2,1)}, u32[]{:S(2)}, u32[]{:S(2)}) collective-permute-start(bf16[512,768]{0,1:T(8,128)(2,1)} %get-tuple-element.21), channel_id=1, source_target_pairs={{3,2},{7,6},{11,10},{15,14},{19,18},{23,22},{27,26},{31,30}} | collective-permute-start | bytes 2359304 | tf_op jit(solution)/shard_map/ppermute | solution.py:44
  181.7 46.1 %collective-permute-start.12 = (bf16[512,768]{0,1:T(8,128)(2,1)}, bf16[512,768]{0,1:T(8,128)(2,1)}, u32[]{:S(2)}, u32[]{:S(2)}) collective-permute-start(bf16[512,768]{0,1:T(8,128)(2,1)} %add_convert_fusion.9), channel_id=1, source_target_pairs={{0,1},{1,2},{4,5},{5,6},{8,9},{9,10},{12,13},{13,14},{16,17},{17,1... | collective-permute-start | bytes 2359304 | tf_op jit(solution)/shard_map/ppermute | solution.py:43
  197.8 30.0 %copy-start.1 = (bf16[2048,768]{0,1:T(8,128)(2,1)S(1)}, bf16[2048,768]{0,1:T(8,128)(2,1)}, u32[]{:S(2)}) copy-start(bf16[2048,768]{0,1:T(8,128)(2,1)} %copy-done) | copy-start | bytes 9437188
  197.8 39.1 %collective-permute-start.21 = (bf16[512,768]{0,1:T(8,128)(2,1)}, bf16[512,768]{0,1:T(8,128)(2,1)}, u32[]{:S(2)}, u32[]{:S(2)}) collective-permute-start(bf16[512,768]{0,1:T(8,128)(2,1)} %get-tuple-element.23), channel_id=1, source_target_pairs={{2,1},{3,2},{6,5},{7,6},{10,9},{11,10},{14,13},{15,14},{18,17},{19... | collective-permute-start | bytes 2359304 | tf_op jit(solution)/shard_map/ppermute | solution.py:44
  214.6 30.4 %collective-permute-start.9 = (bf16[512,768]{0,1:T(8,128)(2,1)}, bf16[512,768]{0,1:T(8,128)(2,1)}, u32[]{:S(2)}, u32[]{:S(2)}) collective-permute-start(bf16[512,768]{0,1:T(8,128)(2,1)} %get-tuple-element.15), channel_id=1, source_target_pairs={{2,1},{3,2},{6,5},{7,6},{10,9},{11,10},{14,13},{15,14},{18,17},{19... | collective-permute-start | bytes 2359304 | tf_op jit(solution)/shard_map/ppermute | solution.py:44
  231.0 22.6 %collective-permute-start.15 = (bf16[512,768]{0,1:T(8,128)(2,1)}, bf16[512,768]{0,1:T(8,128)(2,1)}, u32[]{:S(2)}, u32[]{:S(2)}) collective-permute-start(bf16[512,768]{0,1:T(8,128)(2,1)} %get-tuple-element.19), channel_id=1, source_target_pairs={{2,1},{3,2},{6,5},{7,6},{10,9},{11,10},{14,13},{15,14},{18,17},{19... | collective-permute-start | bytes 2359304 | tf_op jit(solution)/shard_map/ppermute | solution.py:44
  232.3 25.8 %collective-permute-start.19 = (bf16[512,768]{0,1:T(8,128)(2,1)}, bf16[512,768]{0,1:T(8,128)(2,1)}, u32[]{:S(2)}, u32[]{:S(2)}) collective-permute-start(bf16[512,768]{0,1:T(8,128)(2,1)} %get-tuple-element.22), channel_id=1, source_target_pairs={{0,1},{1,2},{2,3},{4,5},{5,6},{6,7},{8,9},{9,10},{10,11},{12,13},{... | collective-permute-start | bytes 2359304 | tf_op jit(solution)/shard_map/ppermute | solution.py:43
  239.2 31.3 %collective-permute-start.22 = (bf16[512,768]{0,1:T(8,128)(2,1)}, bf16[512,768]{0,1:T(8,128)(2,1)}, u32[]{:S(2)}, u32[]{:S(2)}) collective-permute-start(bf16[512,768]{0,1:T(8,128)(2,1)} %add_convert_fusion.2), channel_id=1, source_target_pairs={{1,0},{2,1},{3,2},{5,4},{6,5},{7,6},{9,8},{10,9},{11,10},{13,12},{... | collective-permute-start | bytes 2359304 | tf_op jit(solution)/shard_map/ppermute | solution.py:44
  241.3 34.9 %collective-permute-start.7 = (bf16[512,768]{0,1:T(8,128)(2,1)}, bf16[512,768]{0,1:T(8,128)(2,1)}, u32[]{:S(2)}, u32[]{:S(2)}) collective-permute-start(bf16[512,768]{0,1:T(8,128)(2,1)} %get-tuple-element.14), channel_id=1, source_target_pairs={{0,1},{1,2},{2,3},{4,5},{5,6},{6,7},{8,9},{9,10},{10,11},{12,13},{... | collective-permute-start | bytes 2359304 | tf_op jit(solution)/shard_map/ppermute | solution.py:43
  247.5 39.9 %collective-permute-start.10 = (bf16[512,768]{0,1:T(8,128)(2,1)}, bf16[512,768]{0,1:T(8,128)(2,1)}, u32[]{:S(2)}, u32[]{:S(2)}) collective-permute-start(bf16[512,768]{0,1:T(8,128)(2,1)} %add_convert_fusion.10), channel_id=1, source_target_pairs={{1,0},{2,1},{3,2},{5,4},{6,5},{7,6},{9,8},{10,9},{11,10},{13,12},{... | collective-permute-start | bytes 2359304 | tf_op jit(solution)/shard_map/ppermute | solution.py:44
  253.7 39.6 %collective-permute-start.13 = (bf16[512,768]{0,1:T(8,128)(2,1)}, bf16[512,768]{0,1:T(8,128)(2,1)}, u32[]{:S(2)}, u32[]{:S(2)}) collective-permute-start(bf16[512,768]{0,1:T(8,128)(2,1)} %get-tuple-element.18), channel_id=1, source_target_pairs={{0,1},{1,2},{2,3},{4,5},{5,6},{6,7},{8,9},{9,10},{10,11},{12,13},{... | collective-permute-start | bytes 2359304 | tf_op jit(solution)/shard_map/ppermute | solution.py:43
  258.1 45.1 %collective-permute-start.16 = (bf16[512,768]{0,1:T(8,128)(2,1)}, bf16[512,768]{0,1:T(8,128)(2,1)}, u32[]{:S(2)}, u32[]{:S(2)}) collective-permute-start(bf16[512,768]{0,1:T(8,128)(2,1)} %add_convert_fusion.6), channel_id=1, source_target_pairs={{1,0},{2,1},{3,2},{5,4},{6,5},{7,6},{9,8},{10,9},{11,10},{13,12},{... | collective-permute-start | bytes 2359304 | tf_op jit(solution)/shard_map/ppermute | solution.py:44
  (11 other events, 118.7 us)
Sparse Core Ops, SparseCore 0:
  9.8 36.4 all-gather.3
  48.2 35.2 all-gather.5
  114.5 24.1 reduce-scatter.9
  142.3 35.1 reduce-scatter.5
  181.0 35.1 reduce-scatter.7

commit v3 on v2

--- a/solution.py
+++ b/solution.py
@@ -13,15 +13,24 @@
 
 
 def gather(rows):
-    own = lax.all_gather(rows, "chip", axis=0, tiled=True)
-    return own, lax.ppermute(own, "core", SWAP)
+    n = lax.axis_size("chip")
+    own = [rows] + [
+        lax.ppermute(rows, "chip", [(i, i ^ k) for i in range(n)]) for k in range(1, n)
+    ]
+    own = jnp.concatenate(own, axis=0)
+    return jnp.concatenate([own, lax.ppermute(own, "core", SWAP)], axis=0)
 
 
 def scatter(own, other):
+    n = lax.axis_size("chip")
+    me = lax.axis_index("chip")
     total = own + lax.ppermute(other, "core", SWAP).astype(F32)
-    return lax.psum_scatter(
-        total.astype(other.dtype), "chip", scatter_dimension=0, tiled=True
+    total = total.astype(other.dtype).reshape((n, -1) + own.shape[1:])
+    total = jnp.concatenate(
+        [lax.dynamic_index_in_dim(total, me ^ k, 0, keepdims=False) for k in range(n)],
+        axis=0,
     )
+    return lax.psum_scatter(total, "chip", scatter_dimension=0, tiled=True)
 
 
 def line_scatter(grad):
@@ -51,19 +60,14 @@
     tok_count, top_count = expert_ids.shape
     d = tokens.shape[1]
     chips = lax.axis_size("chip")
-    core = lax.axis_index("core")
-    me = lax.axis_index("chip") * 2 + core
+    me = lax.axis_index("chip") * 2 + lax.axis_index("core")
     local_experts, h = expert_weights.shape[2:]
     half = chips * tok_count
     eh = local_experts * h
 
-    x = jnp.concatenate(gather(tokens), axis=0)
-    g = jnp.concatenate(gather(out_grad), axis=0)
-    small = jnp.concatenate([expert_ids.astype(F32), gate_probs], axis=1)
-    small = lax.all_gather(small, ("chip", "core"), axis=0)
-    small = small.reshape(chips, 2, tok_count, 2 * top_count)
-    small = jnp.where(core == 0, small, small[:, ::-1])
-    small = small.transpose(1, 0, 2, 3).reshape(2 * half, 2 * top_count)
+    x = gather(tokens)
+    small = gather(jnp.concatenate([expert_ids.astype(F32), gate_probs], axis=1))
+    g = gather(out_grad)
     ids = small[:, :top_count].astype(jnp.int32)
     probs = small[:, top_count:]
 

time: 324 us -> 320 us (0.988)
  waiting for transfers between devices: 131 us -> 117 us
  starting transfers between devices: 40.5 us -> 50.8 us
  blocking collectives: 9 us -> 0 us
  local copies, waits for them, and re-layouts: 41.5 us -> 48.7 us
    all_gather x2 -> x0, waiting for transfers between devices: 43.6 us -> none  [gather(): own = lax.all_gather(rows, 'chip', axis=0, tiled=True)]
    ppermute x2 -> x12, waiting for transfers between devices: 0.01 us -> 19.9 us  [the longest x9 19.5 us: gather(): lax.ppermute(rows, 'chip', [(i, i ^ k) for i in range(n)])]
    ppermute x2 -> x12, starting transfers between devices: 0.01 us -> 11.2 us  [the longest x9 10.6 us: gather(): lax.ppermute(rows, 'chip', [(i, i ^ k) for i in range(n)])]
    ppermute x9, waiting for transfers between devices: 55.2 us -> 65.6 us  [line_scatter(): up = lax.ppermute(a.astype(BF16), 'dp', [(i, i + 1) for i in range(t + 1)])]
    all_gather x1 -> x0, blocking collectives: 9 us -> none  [local(): small = lax.all_gather(small, ('chip', 'core'), axis=0)]
    unnamed x34 -> x57, local copies, waits for them, and re-layouts: 5.24 us -> 10.6 us
    concatenate x1 -> x7, other arithmetic: 0.69 us -> 4.21 us  [the longest x3 3.15 us: scatter(): jnp.concatenate([lax.dynamic_index_in_dim(total, me ^ k, 0, keepdims=Fals...]
    ppermute x3, waiting for transfers between devices: 0.01 us -> 3.31 us  [scatter(): total = own + lax.ppermute(other, 'core', SWAP).astype(F32)]
  transfers between devices with their start and end apart: 28 -> 36, of which waited for: 11 -> 15; matrix products, arithmetic and copies ran while one was open for 36% -> 39% of each run, Pallas kernels for 0% -> 0%
where the time goes in v3:
time: 320 us; the launch traced here: 319 us
  waiting for transfers between devices  117 us (37%)
  starting transfers between devices  50.8 us (16%)
  local copies, waits for them, and re-layouts  48.7 us (15%)
  other arithmetic  44.3 us (14%)
  matrix products  43.6 us (14%)
  between operations  14.4 us (4%)
    ppermute x9, waiting for transfers between devices, line_scatter(): up = lax.ppermute(a.astype(BF16), 'dp', [(i, i + 1) for i in range(t + 1)])  65.6 us
    dot_general x9, matrix products, dot(): lax.dot_general(a, b, (((ca,), (cb,)), ((), ())), preferred_element_type=...  43.6 us
    ppermute x9, waiting for transfers between devices, line_scatter(): lax.ppermute(b.astype(BF16), 'dp', [(i, i - 1) for i in range(n - 1 - t,...  28.1 us
    reshape x1, local copies, waits for them, and re-layouts, local(): w = expert_weights.reshape(d, 3 * eh)  20.9 us
    ppermute x9, starting transfers between devices, line_scatter(): up = lax.ppermute(a.astype(BF16), 'dp', [(i, i + 1) for i in range(t + 1)])  19.9 us
    ppermute x9, waiting for transfers between devices, gather(): lax.ppermute(rows, 'chip', [(i, i ^ k) for i in range(n)])  19.5 us
    ppermute x9, starting transfers between devices, line_scatter(): lax.ppermute(b.astype(BF16), 'dp', [(i, i - 1) for i in range(n - 1 - t,...  18.5 us
    convert_element_type x6, other arithmetic, line_scatter(): up = lax.ppermute(a.astype(BF16), 'dp', [(i, i + 1) for i in range(t + 1)])  14.4 us
  transfers between devices with their start and end apart: 36, of which 15 were waited for; matrix products, arithmetic and copies ran while one was open for 39% of the time, Pallas kernels for 0%

profile of v3, /device:TPU:8, one launch (start us, length us, event | category | flops | bytes accessed | tf_op | source)
XLA Modules:
  0.0 318.7 jit_solution(5870284152543806588)
XLA Ops:
  19.4 20.9 %reshape.31 = bf16[2048,2304]{1,0:T(8,128)(2,1)} reshape(bf16[2048,3,2,384]{3,2,1,0:T(2,128)(2,1)} %param.8) | data formatting | bytes 18874368 | tf_op jit(solution)/shard_map/reshape | solution.py:85
  45.1 11.0 %collective-permute-done.11 = bf16[128,2048]{1,0:T(8,128)(2,1)S(1)} collective-permute-done((bf16[128,2048]{1,0:T(8,128)(2,1)S(1)}, bf16[128,2048]{1,0:T(8,128)(2,1)S(1)}, u32[]{:S(2)}, u32[]{:S(2)}) %collective-permute-start.11) | collective-permute-done | bytes 524320 | tf_op jit(solution)/shard_map/ppermute | solution.py:18
  56.1 8.3 %collective-permute-done.10 = bf16[128,2048]{1,0:T(8,128)(2,1)S(1)} collective-permute-done((bf16[128,2048]{1,0:T(8,128)(2,1)S(1)}, bf16[128,2048]{1,0:T(8,128)(2,1)S(1)}, u32[]{:S(2)}, u32[]{:S(2)}) %collective-permute-start.10) | collective-permute-done | bytes 524320 | tf_op jit(solution)/shard_map/ppermute | solution.py:18
  69.1 6.6 %fusion.4 = f32[1024,1536]{1,0:T(8,128)S(1)} fusion(bf16[1024,2048]{1,0:T(8,128)(2,1)S(1)} %constant_dynamic-update-slice_fusion.5, bf16[2048,2304]{1,0:T(8,128)(2,1)S(1)} %copy-done.3), kind=kOutput, calls=%fused_computation.4 | convolution fusion | flops 6442450944 | bytes 16777216 | tf_op jit(solution)/shard_map/dot_general | solution.py:12
  76.0 3.7 %fusion.37 = (f32[1024,768]{1,0:T(8,128)S(1)}, f32[1024,768]{1,0:T(8,128)S(1)}) fusion(f32[1024,1536]{1,0:T(8,128)S(1)} %fusion.4, bf16[1024,2048]{1,0:T(8,128)(2,1)S(1)} %constant_dynamic-update-slice_fusion.10, bf16[2048,2304]{1,0:T(8,128)(2,1)S(1)} %copy-done.3), kind=kOutput, calls=%fused_computation.105 | convolution fusion | flops 3225944064 | bytes 19922944 | tf_op jit(solution)/shard_map/dot_general | solution.py:12
  86.6 4.7 %fusion.9 = bf16[512,2048]{1,0:T(8,128)(2,1)} fusion(bf16[2048,2304]{1,0:T(8,128)(2,1)S(1)} %copy-done.3, bf16[1024,768]{1,0:T(8,128)(2,1)S(1)} %get-tuple-element.12, bf16[1024,768]{1,0:T(8,128)(2,1)S(1)} %get-tuple-element.11), kind=kOutput, calls=%fused_computation.22 | convolution fusion | flops 3225419776 | bytes 11534336 | tf_op jit(solution)/shard_map/dot_general | solution.py:12
  91.8 3.3 %collective-permute-done.14 = f32[512,4]{0,1:T(4,128)S(1)} collective-permute-done((f32[512,4]{0,1:T(4,128)S(1)}, f32[512,4]{0,1:T(4,128)S(1)}, u32[]{:S(2)}, u32[]{:S(2)}) %collective-permute-start.14) | collective-permute-done | bytes 8224 | tf_op jit(solution)/shard_map/ppermute | solution.py:27
  96.1 4.7 %add_convert_fusion.1 = bf16[512,2048]{1,0:T(8,128)(2,1)S(1)} fusion(bf16[512,2048]{1,0:T(8,128)(2,1)} %collective-permute-done.8, bf16[2048,2304]{1,0:T(8,128)(2,1)} %reshape.31, bf16[1024,768]{1,0:T(8,128)(2,1)} %copy-done.14), kind=kOutput, calls=%fused_computation.8 | convolution fusion | flops 1613758464 | bytes 8126464 | tf_op jit(solution)/shard_map/dot_general | solution.py:12
  100.8 6.9 %add_convert_fusion = bf16[512,2048]{1,0:T(8,128)(2,1)S(1)} fusion(bf16[512,2048]{1,0:T(8,128)(2,1)} %collective-permute-done.13, bf16[2048,2304]{1,0:T(8,128)(2,1)} %reshape.31, bf16[1024,768]{1,0:T(8,128)(2,1)S(1)} %get-tuple-element.11, bf16[1024,768]{1,0:T(8,128)(2,1)S(1)} %get-tuple-element.12), kind=kOutput, calls=%fused_computation.7 | convolution fusion | flops 3227516928 | bytes 13631488 | tf_op jit(solution)/shard_map/dot_general | solution.py:12
  111.1 6.1 %convolution_convert_fusion = bf16[2048,768]{0,1:T(8,128)(2,1)S(1)} fusion(bf16[1024,2048]{1,0:T(8,128)(2,1)} %copy-done.20, bf16[1024,768]{1,0:T(8,128)(2,1)S(1)} %copy-done.15), kind=kOutput, calls=%fused_computation.9 | convolution fusion | flops 3222798336 | bytes 8912896 | tf_op jit(solution)/shard_map/dot_general | solution.py:12
  119.8 3.9 %convolution_convert_fusion.2 = bf16[2048,768]{0,1:T(8,128)(2,1)S(1)} fusion(bf16[1024,2048]{1,0:T(8,128)(2,1)S(1)} %copy-done.18, bf16[1024,768]{1,0:T(8,128)(2,1)S(1)} %get-tuple-element.11), kind=kOutput, calls=%fused_computation.11 | convolution fusion | flops 3222798336 | bytes 8912896 | tf_op jit(solution)/shard_map/dot_general | solution.py:12
  126.2 4.0 %convolution_convert_fusion.1 = bf16[2048,768]{0,1:T(8,128)(2,1)S(1)} fusion(bf16[1024,2048]{1,0:T(8,128)(2,1)S(1)} %copy-done.18, bf16[1024,768]{1,0:T(8,128)(2,1)S(1)} %copy-done.13), kind=kOutput, calls=%fused_computation.10 | convolution fusion | flops 3222798336 | bytes 8912896 | tf_op jit(solution)/shard_map/dot_general | solution.py:12
  136.1 4.6 %collective-permute-done.27 = bf16[512,768]{0,1:T(8,128)(2,1)S(1)} collective-permute-done((bf16[512,768]{0,1:T(8,128)(2,1)S(1)}, bf16[512,768]{0,1:T(8,128)(2,1)S(1)}, u32[]{:S(2)}, u32[]{:S(2)}) %collective-permute-start.27) | collective-permute-done | bytes 786464 | tf_op jit(solution)/shard_map/ppermute | solution.py:52
  143.8 13.8 %collective-permute-done.15 = bf16[512,768]{0,1:T(8,128)(2,1)S(1)} collective-permute-done((bf16[512,768]{0,1:T(8,128)(2,1)S(1)}, bf16[512,768]{0,1:T(8,128)(2,1)S(1)}, u32[]{:S(2)}, u32[]{:S(2)}) %collective-permute-start.15) | collective-permute-done | bytes 786464 | tf_op jit(solution)/shard_map/ppermute | solution.py:52
  162.3 12.2 %collective-permute-done.21 = bf16[512,768]{0,1:T(8,128)(2,1)} collective-permute-done((bf16[512,768]{0,1:T(8,128)(2,1)}, bf16[512,768]{0,1:T(8,128)(2,1)}, u32[]{:S(2)}, u32[]{:S(2)}) %collective-permute-start.21) | collective-permute-done | bytes 786464 | tf_op jit(solution)/shard_map/ppermute | solution.py:52
  180.3 11.0 %collective-permute-done.28 = bf16[512,768]{0,1:T(8,128)(2,1)} collective-permute-done((bf16[512,768]{0,1:T(8,128)(2,1)}, bf16[512,768]{0,1:T(8,128)(2,1)}, u32[]{:S(2)}, u32[]{:S(2)}) %collective-permute-start.28) | collective-permute-done | bytes 786464 | tf_op jit(solution)/shard_map/ppermute | solution.py:52
  191.4 3.4 %add_convert_fusion.4 = (bf16[512,768]{0,1:T(8,128)(2,1)}, bf16[512,768]{0,1:T(8,128)(2,1)}) fusion(bf16[512,768]{0,1:T(8,128)(2,1)} %collective-permute-done.28, bf16[2048,768]{0,1:T(8,128)(2,1)} %copy-done.2, s32[]{:T(128)S(6)} %select_n.80, bf16[512,768]{0,1:T(8,128)(2,1)} %collective-permute-done.30, s32[]{:T(128)S(6)} %select_n.84), kind=kLoop, calls=%fused_computation.41 | loop fusion | flops 3145728 | bytes 4718600 | tf_op jit(solution)/shard_map/convert_element_type | solution.py:52
  196.1 12.1 %collective-permute-done.16 = bf16[512,768]{0,1:T(8,128)(2,1)} collective-permute-done((bf16[512,768]{0,1:T(8,128)(2,1)}, bf16[512,768]{0,1:T(8,128)(2,1)}, u32[]{:S(2)}, u32[]{:S(2)}) %collective-permute-start.16) | collective-permute-done | bytes 786464 | tf_op jit(solution)/shard_map/ppermute | solution.py:52
  208.2 3.2 add_convert_fusion.12
  212.7 11.8 %collective-permute-done.22 = bf16[512,768]{0,1:T(8,128)(2,1)} collective-permute-done((bf16[512,768]{0,1:T(8,128)(2,1)}, bf16[512,768]{0,1:T(8,128)(2,1)}, u32[]{:S(2)}, u32[]{:S(2)}) %collective-permute-start.22) | collective-permute-done | bytes 786464 | tf_op jit(solution)/shard_map/ppermute | solution.py:52
  228.9 4.6 %collective-permute-start.29 = (bf16[512,768]{0,1:T(8,128)(2,1)}, bf16[512,768]{0,1:T(8,128)(2,1)}, u32[]{:S(2)}, u32[]{:S(2)}) collective-permute-start(bf16[512,768]{0,1:T(8,128)(2,1)} %get-tuple-element.22), channel_id=1, source_target_pairs={{0,1},{1,2},{2,3},{4,5},{5,6},{6,7},{8,9},{9,10},{10,11},{12,13},{... | collective-permute-start | bytes 2359304 | tf_op jit(solution)/shard_map/ppermute | solution.py:52
  238.2 3.6 %collective-permute-start.17 = (bf16[512,768]{0,1:T(8,128)(2,1)}, bf16[512,768]{0,1:T(8,128)(2,1)}, u32[]{:S(2)}, u32[]{:S(2)}) collective-permute-start(bf16[512,768]{0,1:T(8,128)(2,1)} %get-tuple-element.14), channel_id=1, source_target_pairs={{0,1},{1,2},{2,3},{4,5},{5,6},{6,7},{8,9},{9,10},{10,11},{12,13},{... | collective-permute-start | bytes 2359304 | tf_op jit(solution)/shard_map/ppermute | solution.py:52
  254.5 4.8 %collective-permute-start.26 = (bf16[512,768]{0,1:T(8,128)(2,1)}, bf16[512,768]{0,1:T(8,128)(2,1)}, u32[]{:S(2)}, u32[]{:S(2)}) collective-permute-start(bf16[512,768]{0,1:T(8,128)(2,1)} %add_convert_fusion.6), channel_id=1, source_target_pairs={{1,0},{2,1},{3,2},{5,4},{6,5},{7,6},{9,8},{10,9},{11,10},{13,12},{... | collective-permute-start | bytes 2359304 | tf_op jit(solution)/shard_map/ppermute | solution.py:53
  260.8 6.3 %collective-permute-done.32 = bf16[512,768]{0,1:T(8,128)(2,1)} collective-permute-done((bf16[512,768]{0,1:T(8,128)(2,1)}, bf16[512,768]{0,1:T(8,128)(2,1)}, u32[]{:S(2)}, u32[]{:S(2)}) %collective-permute-start.32) | collective-permute-done | bytes 786464 | tf_op jit(solution)/shard_map/ppermute | solution.py:53
  267.1 3.2 convert_add_fusion
  270.3 3.6 %copy.26 = f32[512,1,2,384]{3,2,1,0:T(2,128)} copy(f32[512,1,2,384]{0,3,2,1:T(8,128)} %bitcast.44) | data formatting | bytes 3145728 | tf_op jit(solution)/shard_map/stack | solution.py:118
  273.9 10.0 %collective-permute-done.20 = bf16[512,768]{0,1:T(8,128)(2,1)} collective-permute-done((bf16[512,768]{0,1:T(8,128)(2,1)}, bf16[512,768]{0,1:T(8,128)(2,1)}, u32[]{:S(2)}, u32[]{:S(2)}) %collective-permute-start.20) | collective-permute-done | bytes 786464 | tf_op jit(solution)/shard_map/ppermute | solution.py:53
  284.0 3.2 convert_add_fusion.2
  287.2 3.7 %copy.24 = f32[512,1,2,384]{3,2,1,0:T(2,128)} copy(f32[512,1,2,384]{0,3,2,1:T(8,128)} %bitcast.45) | data formatting | bytes 3145728 | tf_op jit(solution)/shard_map/stack | solution.py:118
  290.9 8.9 %collective-permute-done.26 = bf16[512,768]{0,1:T(8,128)(2,1)} collective-permute-done((bf16[512,768]{0,1:T(8,128)(2,1)}, bf16[512,768]{0,1:T(8,128)(2,1)}, u32[]{:S(2)}, u32[]{:S(2)}) %collective-permute-start.26) | collective-permute-done | bytes 786464 | tf_op jit(solution)/shard_map/ppermute | solution.py:53
  302.6 3.9 %copy.25 = f32[512,1,2,384]{3,2,1,0:T(2,128)} copy(f32[512,1,2,384]{0,3,2,1:T(8,128)} %bitcast.43) | data formatting | bytes 3145728 | tf_op jit(solution)/shard_map/stack | solution.py:118
  306.5 5.7 %pad_maximum_fusion = f32[512,3,2,384]{3,2,1,0:T(2,128)} fusion(f32[512,1,2,384]{3,2,1,0:T(2,128)S(1)} %copy-done.4, f32[512,1,2,384]{3,2,1,0:T(2,128)} %copy.25, f32[512,1,2,384]{3,2,1,0:T(2,128)S(1)} %copy-done.5), kind=kLoop, calls=%fused_computation.6 | loop fusion | flops 2359296 | bytes 9437184 | tf_op jit(solution)/shard_map/stack | solution.py:118
  (150 shorter events, 86.8 us)
Async XLA Ops:
  7.2 252.1 %reduce-scatter.10.cloned.1.call-start = ((), (), s32[]{:S(2)}) async-start(), calls=%async_computation.5 | async-start | bytes 327680
  10.1 30.1 %collective-permute-start = (f32[128,8]{0,1:T(8,128)S(1)}, f32[128,8]{0,1:T(8,128)S(1)}, u32[]{:S(2)}, u32[]{:S(2)}) collective-permute-start(f32[128,8]{0,1:T(8,128)S(1)} %get-tuple-element.38), channel_id=1, source_target_pairs={{0,8},{8,0},{16,24},{24,16},{1,9},{9,1},{17,25},{25,17},{2,10},{10... | collective-permute-start | bytes 12296 | tf_op jit(solution)/shard_map/ppermute | solution.py:18
  11.6 31.7 %collective-permute-start.6 = (bf16[128,2048]{1,0:T(8,128)(2,1)}, bf16[128,2048]{1,0:T(8,128)(2,1)S(1)}, u32[]{:S(2)}, u32[]{:S(2)}) collective-permute-start(bf16[128,2048]{1,0:T(8,128)(2,1)} %param.5), channel_id=1, source_target_pairs={{0,24},{8,16},{16,8},{24,0},{1,25},{9,17},{17,9},{25,1},{2,26},{10... | collective-permute-start | bytes 1572872 | tf_op jit(solution)/shard_map/ppermute | solution.py:18
  12.1 31.8 %collective-permute-start.5 = (bf16[128,2048]{1,0:T(8,128)(2,1)}, bf16[128,2048]{1,0:T(8,128)(2,1)S(1)}, u32[]{:S(2)}, u32[]{:S(2)}) collective-permute-start(bf16[128,2048]{1,0:T(8,128)(2,1)} %param.5), channel_id=1, source_target_pairs={{0,16},{8,24},{16,0},{24,8},{1,17},{9,25},{17,1},{25,9},{2,18},{10... | collective-permute-start | bytes 1572872 | tf_op jit(solution)/shard_map/ppermute | solution.py:18
  13.6 30.3 %collective-permute-start.4 = (bf16[128,2048]{1,0:T(8,128)(2,1)}, bf16[128,2048]{1,0:T(8,128)(2,1)S(1)}, u32[]{:S(2)}, u32[]{:S(2)}) collective-permute-start(bf16[128,2048]{1,0:T(8,128)(2,1)} %param.5), channel_id=1, source_target_pairs={{0,8},{8,0},{16,24},{24,16},{1,9},{9,1},{17,25},{25,17},{2,10},{10... | collective-permute-start | bytes 1572872 | tf_op jit(solution)/shard_map/ppermute | solution.py:18
  17.0 25.8 %collective-permute-start.2 = (f32[128,8]{0,1:T(8,128)S(1)}, f32[128,8]{0,1:T(8,128)S(1)}, u32[]{:S(2)}, u32[]{:S(2)}) collective-permute-start(f32[128,8]{0,1:T(8,128)S(1)} %get-tuple-element.38), channel_id=1, source_target_pairs={{0,24},{8,16},{16,8},{24,0},{1,25},{9,17},{17,9},{25,1},{2,26},{10... | collective-permute-start | bytes 12296 | tf_op jit(solution)/shard_map/ppermute | solution.py:18
  40.2 15.9 %collective-permute-start.11 = (bf16[128,2048]{1,0:T(8,128)(2,1)S(1)}, bf16[128,2048]{1,0:T(8,128)(2,1)S(1)}, u32[]{:S(2)}, u32[]{:S(2)}) collective-permute-start(bf16[128,2048]{1,0:T(8,128)(2,1)S(1)} %copy-done.11), channel_id=1, source_target_pairs={{0,24},{8,16},{16,8},{24,0},{1,25},{9,17},{17,9},{25,1},{2,26},{10... | collective-permute-start | bytes 1572872 | tf_op jit(solution)/shard_map/ppermute | solution.py:18
  42.8 21.7 %collective-permute-start.10 = (bf16[128,2048]{1,0:T(8,128)(2,1)S(1)}, bf16[128,2048]{1,0:T(8,128)(2,1)S(1)}, u32[]{:S(2)}, u32[]{:S(2)}) collective-permute-start(bf16[128,2048]{1,0:T(8,128)(2,1)S(1)} %copy-done.11), channel_id=1, source_target_pairs={{0,16},{8,24},{16,0},{24,8},{1,17},{9,25},{17,1},{25,9},{2,18},{10... | collective-permute-start | bytes 1572872 | tf_op jit(solution)/shard_map/ppermute | solution.py:18
  43.3 21.2 %collective-permute-start.9 = (bf16[128,2048]{1,0:T(8,128)(2,1)S(1)}, bf16[128,2048]{1,0:T(8,128)(2,1)S(1)}, u32[]{:S(2)}, u32[]{:S(2)}) collective-permute-start(bf16[128,2048]{1,0:T(8,128)(2,1)S(1)} %copy-done.11), channel_id=1, source_target_pairs={{0,8},{8,0},{16,24},{24,16},{1,9},{9,1},{17,25},{25,17},{2,10},{10... | collective-permute-start | bytes 1572872 | tf_op jit(solution)/shard_map/ppermute | solution.py:18
  44.1 23.5 %collective-permute-start.7 = (bf16[512,2048]{1,0:T(8,128)(2,1)S(1)}, bf16[512,2048]{1,0:T(8,128)(2,1)S(1)}, u32[]{:S(2)}, u32[]{:S(2)}) collective-permute-start(bf16[512,2048]{1,0:T(8,128)(2,1)S(1)} %pad_maximum_fusion.2), channel_id=1, source_target_pairs={{0,4},{4,0},{1,5},{5,1},{2,6},{6,2},{3,7},{7,3},{8,12},{12,8},{9,1... | collective-permute-start | bytes 6291464 | tf_op jit(solution)/shard_map/ppermute | solution.py:21
  64.8 11.0 %collective-permute-start.12 = (bf16[512,2048]{1,0:T(8,128)(2,1)S(1)}, bf16[512,2048]{1,0:T(8,128)(2,1)S(1)}, u32[]{:S(2)}, u32[]{:S(2)}) collective-permute-start(bf16[512,2048]{1,0:T(8,128)(2,1)S(1)} %pad_maximum_fusion.4), channel_id=1, source_target_pairs={{0,4},{4,0},{1,5},{5,1},{2,6},{6,2},{3,7},{7,3},{8,12},{12,8},{9,1... | collective-permute-start | bytes 6291464 | tf_op jit(solution)/shard_map/ppermute | solution.py:21
  86.1 9.9 %collective-permute-start.8 = (bf16[512,2048]{1,0:T(8,128)(2,1)}, bf16[512,2048]{1,0:T(8,128)(2,1)}, u32[]{:S(2)}, u32[]{:S(2)}) collective-permute-start(bf16[512,2048]{1,0:T(8,128)(2,1)} %convolution_convert_fusion.3), channel_id=1, source_target_pairs={{0,4},{4,0},{1,5},{5,1},{2,6},{6,2},{3,7},{7,3},{8,12},{12,8},{9,1... | collective-permute-start | bytes 6291464 | tf_op jit(solution)/shard_map/ppermute | solution.py:27
  96.0 216.1 %reduce-scatter.8.cloned.1.call-start = ((), (), s32[]{:S(2)}) async-start(), calls=%async_computation.4 | async-start | bytes 2621440 | tf_op jit(solution)/shard_map/reduce_scatter | solution.py:33
  110.7 201.4 %reduce-scatter.6.cloned.1.call-start = ((), (), s32[]{:S(2)}) async-start(), calls=%async_computation.3 | async-start | bytes 2621440 | tf_op jit(solution)/shard_map/reduce_scatter | solution.py:33
  118.5 22.3 %collective-permute-start.27 = (bf16[512,768]{0,1:T(8,128)(2,1)S(1)}, bf16[512,768]{0,1:T(8,128)(2,1)S(1)}, u32[]{:S(2)}, u32[]{:S(2)}) collective-permute-start(bf16[512,768]{0,1:T(8,128)(2,1)S(1)} %get-tuple-element.24), channel_id=1, source_target_pairs={{0,1},{4,5},{8,9},{12,13},{16,17},{20,21},{24,25},{28,29}} | collective-permute-start | bytes 2359304 | tf_op jit(solution)/shard_map/ppermute | solution.py:52
  124.7 32.9 %collective-permute-start.15 = (bf16[512,768]{0,1:T(8,128)(2,1)S(1)}, bf16[512,768]{0,1:T(8,128)(2,1)S(1)}, u32[]{:S(2)}, u32[]{:S(2)}) collective-permute-start(bf16[512,768]{0,1:T(8,128)(2,1)S(1)} %get-tuple-element.16), channel_id=1, source_target_pairs={{0,1},{4,5},{8,9},{12,13},{16,17},{20,21},{24,25},{28,29}} | collective-permute-start | bytes 2359304 | tf_op jit(solution)/shard_map/ppermute | solution.py:52
  130.2 48.2 %collective-permute-start.30 = (bf16[512,768]{0,1:T(8,128)(2,1)}, bf16[512,768]{0,1:T(8,128)(2,1)}, u32[]{:S(2)}, u32[]{:S(2)}) collective-permute-start(bf16[512,768]{0,1:T(8,128)(2,1)} %get-tuple-element.25), channel_id=1, source_target_pairs={{3,2},{7,6},{11,10},{15,14},{19,18},{23,22},{27,26},{31,30}} | collective-permute-start | bytes 2359304 | tf_op jit(solution)/shard_map/ppermute | solution.py:53
  131.7 64.4 %collective-permute-start.18 = (bf16[512,768]{0,1:T(8,128)(2,1)}, bf16[512,768]{0,1:T(8,128)(2,1)}, u32[]{:S(2)}, u32[]{:S(2)}) collective-permute-start(bf16[512,768]{0,1:T(8,128)(2,1)} %get-tuple-element.17), channel_id=1, source_target_pairs={{3,2},{7,6},{11,10},{15,14},{19,18},{23,22},{27,26},{31,30}} | collective-permute-start | bytes 2359304 | tf_op jit(solution)/shard_map/ppermute | solution.py:53
  134.7 39.9 %collective-permute-start.21 = (bf16[512,768]{0,1:T(8,128)(2,1)}, bf16[512,768]{0,1:T(8,128)(2,1)}, u32[]{:S(2)}, u32[]{:S(2)}) collective-permute-start(bf16[512,768]{0,1:T(8,128)(2,1)} %get-tuple-element.20), channel_id=1, source_target_pairs={{0,1},{4,5},{8,9},{12,13},{16,17},{20,21},{24,25},{28,29}} | collective-permute-start | bytes 2359304 | tf_op jit(solution)/shard_map/ppermute | solution.py:52
  141.9 49.5 %collective-permute-start.28 = (bf16[512,768]{0,1:T(8,128)(2,1)}, bf16[512,768]{0,1:T(8,128)(2,1)}, u32[]{:S(2)}, u32[]{:S(2)}) collective-permute-start(bf16[512,768]{0,1:T(8,128)(2,1)} %add_convert_fusion.5), channel_id=1, source_target_pairs={{0,1},{1,2},{4,5},{5,6},{8,9},{9,10},{12,13},{13,14},{16,17},{17,1... | collective-permute-start | bytes 2359304 | tf_op jit(solution)/shard_map/ppermute | solution.py:52
  158.8 49.5 %collective-permute-start.16 = (bf16[512,768]{0,1:T(8,128)(2,1)}, bf16[512,768]{0,1:T(8,128)(2,1)}, u32[]{:S(2)}, u32[]{:S(2)}) collective-permute-start(bf16[512,768]{0,1:T(8,128)(2,1)} %add_convert_fusion.13), channel_id=1, source_target_pairs={{0,1},{1,2},{4,5},{5,6},{8,9},{9,10},{12,13},{13,14},{16,17},{17,1... | collective-permute-start | bytes 2359304 | tf_op jit(solution)/shard_map/ppermute | solution.py:52
  174.5 38.2 %collective-permute-start.24 = (bf16[512,768]{0,1:T(8,128)(2,1)}, bf16[512,768]{0,1:T(8,128)(2,1)}, u32[]{:S(2)}, u32[]{:S(2)}) collective-permute-start(bf16[512,768]{0,1:T(8,128)(2,1)} %get-tuple-element.21), channel_id=1, source_target_pairs={{3,2},{7,6},{11,10},{15,14},{19,18},{23,22},{27,26},{31,30}} | collective-permute-start | bytes 2359304 | tf_op jit(solution)/shard_map/ppermute | solution.py:53
  178.4 46.1 %collective-permute-start.22 = (bf16[512,768]{0,1:T(8,128)(2,1)}, bf16[512,768]{0,1:T(8,128)(2,1)}, u32[]{:S(2)}, u32[]{:S(2)}) collective-permute-start(bf16[512,768]{0,1:T(8,128)(2,1)} %add_convert_fusion.9), channel_id=1, source_target_pairs={{0,1},{1,2},{4,5},{5,6},{8,9},{9,10},{12,13},{13,14},{16,17},{17,1... | collective-permute-start | bytes 2359304 | tf_op jit(solution)/shard_map/ppermute | solution.py:52
  194.8 38.6 %collective-permute-start.31 = (bf16[512,768]{0,1:T(8,128)(2,1)}, bf16[512,768]{0,1:T(8,128)(2,1)}, u32[]{:S(2)}, u32[]{:S(2)}) collective-permute-start(bf16[512,768]{0,1:T(8,128)(2,1)} %get-tuple-element.23), channel_id=1, source_target_pairs={{2,1},{3,2},{6,5},{7,6},{10,9},{11,10},{14,13},{15,14},{18,17},{19... | collective-permute-start | bytes 2359304 | tf_op jit(solution)/shard_map/ppermute | solution.py:53
  211.4 30.5 %collective-permute-start.19 = (bf16[512,768]{0,1:T(8,128)(2,1)}, bf16[512,768]{0,1:T(8,128)(2,1)}, u32[]{:S(2)}, u32[]{:S(2)}) collective-permute-start(bf16[512,768]{0,1:T(8,128)(2,1)} %get-tuple-element.15), channel_id=1, source_target_pairs={{2,1},{3,2},{6,5},{7,6},{10,9},{11,10},{14,13},{15,14},{18,17},{19... | collective-permute-start | bytes 2359304 | tf_op jit(solution)/shard_map/ppermute | solution.py:53
  227.6 22.7 %collective-permute-start.25 = (bf16[512,768]{0,1:T(8,128)(2,1)}, bf16[512,768]{0,1:T(8,128)(2,1)}, u32[]{:S(2)}, u32[]{:S(2)}) collective-permute-start(bf16[512,768]{0,1:T(8,128)(2,1)} %get-tuple-element.19), channel_id=1, source_target_pairs={{2,1},{3,2},{6,5},{7,6},{10,9},{11,10},{14,13},{15,14},{18,17},{19... | collective-permute-start | bytes 2359304 | tf_op jit(solution)/shard_map/ppermute | solution.py:53
  228.9 25.6 %collective-permute-start.29 = (bf16[512,768]{0,1:T(8,128)(2,1)}, bf16[512,768]{0,1:T(8,128)(2,1)}, u32[]{:S(2)}, u32[]{:S(2)}) collective-permute-start(bf16[512,768]{0,1:T(8,128)(2,1)} %get-tuple-element.22), channel_id=1, source_target_pairs={{0,1},{1,2},{2,3},{4,5},{5,6},{6,7},{8,9},{9,10},{10,11},{12,13},{... | collective-permute-start | bytes 2359304 | tf_op jit(solution)/shard_map/ppermute | solution.py:52
  236.0 31.1 %collective-permute-start.32 = (bf16[512,768]{0,1:T(8,128)(2,1)}, bf16[512,768]{0,1:T(8,128)(2,1)}, u32[]{:S(2)}, u32[]{:S(2)}) collective-permute-start(bf16[512,768]{0,1:T(8,128)(2,1)} %add_convert_fusion.2), channel_id=1, source_target_pairs={{1,0},{2,1},{3,2},{5,4},{6,5},{7,6},{9,8},{10,9},{11,10},{13,12},{... | collective-permute-start | bytes 2359304 | tf_op jit(solution)/shard_map/ppermute | solution.py:53
  238.2 35.7 %collective-permute-start.17 = (bf16[512,768]{0,1:T(8,128)(2,1)}, bf16[512,768]{0,1:T(8,128)(2,1)}, u32[]{:S(2)}, u32[]{:S(2)}) collective-permute-start(bf16[512,768]{0,1:T(8,128)(2,1)} %get-tuple-element.14), channel_id=1, source_target_pairs={{0,1},{1,2},{2,3},{4,5},{5,6},{6,7},{8,9},{9,10},{10,11},{12,13},{... | collective-permute-start | bytes 2359304 | tf_op jit(solution)/shard_map/ppermute | solution.py:52
  244.3 39.7 %collective-permute-start.20 = (bf16[512,768]{0,1:T(8,128)(2,1)}, bf16[512,768]{0,1:T(8,128)(2,1)}, u32[]{:S(2)}, u32[]{:S(2)}) collective-permute-start(bf16[512,768]{0,1:T(8,128)(2,1)} %add_convert_fusion.10), channel_id=1, source_target_pairs={{1,0},{2,1},{3,2},{5,4},{6,5},{7,6},{9,8},{10,9},{11,10},{13,12},{... | collective-permute-start | bytes 2359304 | tf_op jit(solution)/shard_map/ppermute | solution.py:53
  250.3 40.6 %collective-permute-start.23 = (bf16[512,768]{0,1:T(8,128)(2,1)}, bf16[512,768]{0,1:T(8,128)(2,1)}, u32[]{:S(2)}, u32[]{:S(2)}) collective-permute-start(bf16[512,768]{0,1:T(8,128)(2,1)} %get-tuple-element.18), channel_id=1, source_target_pairs={{0,1},{1,2},{2,3},{4,5},{5,6},{6,7},{8,9},{9,10},{10,11},{12,13},{... | collective-permute-start | bytes 2359304 | tf_op jit(solution)/shard_map/ppermute | solution.py:52
  254.5 45.2 %collective-permute-start.26 = (bf16[512,768]{0,1:T(8,128)(2,1)}, bf16[512,768]{0,1:T(8,128)(2,1)}, u32[]{:S(2)}, u32[]{:S(2)}) collective-permute-start(bf16[512,768]{0,1:T(8,128)(2,1)} %add_convert_fusion.6), channel_id=1, source_target_pairs={{1,0},{2,1},{3,2},{5,4},{6,5},{7,6},{9,8},{10,9},{11,10},{13,12},{... | collective-permute-start | bytes 2359304 | tf_op jit(solution)/shard_map/ppermute | solution.py:53
  (26 other events, 365.7 us)
Sparse Core Ops, SparseCore 0:
  96.1 24.4 reduce-scatter.9
  124.5 35.1 reduce-scatter.7
  163.2 35.1 reduce-scatter.5
